TPU v7x, 128 devices: a whole 4x4x4 slice. The times are simulated.
128 devices in a mesh: ctx: 16 (over y, z), head: 8 (over x, core).
Axes of the slice: x: 4, y: 4, z: 4, core: 2. Of those that a mesh axis runs over, the one named last changes fastest.
Arguments:
- queries: bfloat16 [16384, 64, 128], P('ctx', 'head'), may hold values from -8 to 8
- key_rows: bfloat16 [16384, 64, 128], P('ctx', 'head'), may hold values from -4 to 4
- value_rows: bfloat16 [16384, 64, 128], P('ctx', 'head'), may hold values from -12 to 12
- grad_normed: bfloat16 [16384, 64, 128], P('ctx', 'head'), may hold values from -6 to 6
- norm_gain: float32 [64, 128], P('head'), may hold values from 0.1 to 1.9
- document_starts: int32 [6], replicated, may hold values from 0 to 16256, as said below
Outputs:
- normed: bfloat16 [16384, 64, 128], P('ctx', 'head')
- grad_queries: bfloat16 [16384, 64, 128], P('ctx', 'head')
- grad_keys: bfloat16 [16384, 64, 128], P('ctx', 'head')
- grad_values: bfloat16 [16384, 64, 128], P('ctx', 'head')
- grad_gain: float32 [64, 128], P('head')
Inputs may be any that keep to these rules, and one draw needn't show every extreme that they name: `document_starts`: strictly increasing multiples of 128; the first is 0 and the last is 16256.
All inputs are finite; a program needn't handle non-finite values.
Results may differ from a plain program's by a relative error of at most 0.0057.
Values sent between devices are 32-bit elements; how exact they have to be, the bound alone decides.
A program may use at most 128 MiB of HBM per device.

v0:
```python
import math

import jax
import jax.numpy as jnp
from jax import lax
from jax.sharding import PartitionSpec as P

HEADS = 64
HEAD_DIM = 128
TILE = 512


EPSILON = 1e-06


def prefix(part, axis, combine, identity, reverse):
    count = lax.axis_size(axis)
    place = lax.axis_index(axis)
    ahead = count - 1 - place if reverse else place
    gathered = jax.tree.map(lambda a: lax.all_gather(a, axis), part)
    state = jax.tree.map(lambda a, e: jnp.zeros_like(a) + jnp.asarray(e, a.dtype), part, identity)

    def one(turn, state):
        source = count - 1 - turn if reverse else turn
        return combine(
            state, jax.tree.map(lambda a: lax.dynamic_index_in_dim(a, source, 0, False), gathered)
        )

    return lax.fori_loop(0, ahead, one, state)


def token_documents(starts, positions):
    return jnp.sum((starts[None, :] <= positions[:, None]).astype(jnp.int32), axis=1) - 1


def chain_state(earlier, later):
    return (later[0] + (1.0 - later[1]) * earlier[0], jnp.maximum(earlier[1], later[1]))


def local(queries, key_rows, value_rows, grad_normed, norm_gain, document_starts):
    shard_rows, local_heads, head_width = queries.shape
    tile_count = shard_rows // TILE
    shard_count = lax.axis_size("ctx")
    shard_index = lax.axis_index("ctx")
    feature_count = HEADS * HEAD_DIM
    first_row = shard_index * shard_rows
    positions = first_row + jnp.arange(shard_rows, dtype=jnp.int32)
    documents = token_documents(document_starts, positions).reshape(tile_count, TILE)
    tile_first = first_row + jnp.arange(tile_count, dtype=jnp.int32) * TILE
    prior_docs = token_documents(document_starts, tile_first - 1)
    last_docs = documents[:, -1]
    entering = (documents == prior_docs[:, None]).astype(jnp.float32)
    leaving = (documents == last_docs[:, None]).astype(jnp.float32)
    keep_flags = (last_docs == prior_docs).astype(jnp.float32)
    causal = jnp.arange(TILE)[:, None] >= jnp.arange(TILE)[None, :]
    within = (causal[None] & (documents[:, :, None] == documents[:, None, :])).astype(jnp.float32)[
        :, None
    ]
    enter_col = entering[:, :, None, None]
    leave_col = leaving[:, :, None, None]
    tiled_query = queries.reshape(tile_count, TILE, local_heads, head_width)
    tiled_key = key_rows.reshape(tile_count, TILE, local_heads, head_width)
    tiled_value = value_rows.reshape(tile_count, TILE, local_heads, head_width)
    scores = jnp.einsum(
        "cthd,cshd->chts", tiled_query, tiled_key, preferred_element_type=jnp.float32
    )
    attention = (scores * within).astype(jnp.bfloat16)
    intra_out = jnp.einsum(
        "chts,cshd->cthd", attention, tiled_value, preferred_element_type=jnp.float32
    )
    leave_keys = tiled_key * leave_col.astype(jnp.bfloat16)
    tile_states = jnp.einsum(
        "cthd,cthe->chde", leave_keys, tiled_value, preferred_element_type=jnp.float32
    )
    running = jnp.zeros_like(tile_states[0])
    local_entry = []
    for tile_number in range(tile_count):
        local_entry.append(running)
        running = tile_states[tile_number] + keep_flags[tile_number] * running
    reset_flag = 1.0 - jnp.prod(keep_flags)
    reach_in = jnp.cumprod(jnp.concatenate([jnp.ones((1,), jnp.float32), keep_flags[:-1]]))
    reach_out = jnp.cumprod(jnp.concatenate([keep_flags[1:], jnp.ones((1,), jnp.float32)])[::-1])[
        ::-1
    ]
    empty_state = (jnp.zeros_like(running), jnp.zeros((), jnp.float32))
    incoming = prefix((running, reset_flag), "ctx", chain_state, empty_state, False)[0]
    entry_states = jnp.stack(local_entry) + reach_in[:, None, None, None] * incoming[None]
    entry_bf = entry_states.astype(jnp.bfloat16)
    inter_out = jnp.einsum(
        "cthd,chde->cthe", tiled_query, entry_bf, preferred_element_type=jnp.float32
    )
    attended = intra_out + enter_col * inter_out
    upstream = grad_normed.reshape(tile_count, TILE, local_heads, head_width).astype(jnp.float32)
    weighted = upstream * norm_gain
    local_squares = jnp.sum(attended * attended, axis=(2, 3))
    local_cross = jnp.sum(weighted * attended, axis=(2, 3))
    squares, cross_sum = lax.psum((local_squares, local_cross), "head")
    inverse = 1.0 / jnp.sqrt(squares / feature_count + EPSILON)
    scaled = attended * inverse[:, :, None, None]
    normed = (scaled * norm_gain).astype(jnp.bfloat16)
    grad_att = (
        inverse[:, :, None, None] * weighted
        - attended * (inverse**3 * cross_sum / feature_count)[:, :, None, None]
    ).astype(jnp.bfloat16)
    gain_local = jnp.sum(upstream * scaled, axis=(0, 1))
    grad_gain = lax.psum(gain_local, "ctx") / math.sqrt(shard_rows * shard_count)
    grad_scores = (
        jnp.einsum("cthe,cshe->chts", grad_att, tiled_value, preferred_element_type=jnp.float32)
        * within
    ).astype(jnp.bfloat16)
    query_intra = jnp.einsum(
        "chts,cshd->cthd", grad_scores, tiled_key, preferred_element_type=jnp.float32
    )
    key_intra = jnp.einsum(
        "chts,cthd->cshd", grad_scores, tiled_query, preferred_element_type=jnp.float32
    )
    value_intra = jnp.einsum(
        "chts,cthe->cshe", attention, grad_att, preferred_element_type=jnp.float32
    )
    query_inter = jnp.einsum(
        "cthe,chde->cthd", grad_att, entry_bf, preferred_element_type=jnp.float32
    )
    grad_queries = (query_intra + enter_col * query_inter).astype(jnp.bfloat16)
    enter_queries = tiled_query * enter_col.astype(jnp.bfloat16)
    tile_grads = jnp.einsum(
        "cthd,cthe->chde", enter_queries, grad_att, preferred_element_type=jnp.float32
    )
    later_sum = jnp.zeros_like(tile_grads[0])
    local_exit = [later_sum] * tile_count
    for tile_number in reversed(range(tile_count)):
        local_exit[tile_number] = later_sum
        later_sum = tile_grads[tile_number] + keep_flags[tile_number] * later_sum
    outgoing = prefix((later_sum, reset_flag), "ctx", chain_state, empty_state, True)[0]
    exit_states = jnp.stack(local_exit) + reach_out[:, None, None, None] * outgoing[None]
    exit_bf = exit_states.astype(jnp.bfloat16)
    key_inter = jnp.einsum(
        "cthe,chde->cthd", tiled_value, exit_bf, preferred_element_type=jnp.float32
    )
    value_inter = jnp.einsum(
        "cthd,chde->cthe", tiled_key, exit_bf, preferred_element_type=jnp.float32
    )
    grad_keys = (key_intra + leave_col * key_inter).astype(jnp.bfloat16)
    grad_values = (value_intra + leave_col * value_inter).astype(jnp.bfloat16)
    whole = (shard_rows, local_heads, head_width)
    return (
        normed.reshape(whole),
        grad_queries.reshape(whole),
        grad_keys.reshape(whole),
        grad_values.reshape(whole),
        grad_gain,
    )


def solution(mesh):
    in_specs = (
        P("ctx", "head", None),
        P("ctx", "head", None),
        P("ctx", "head", None),
        P("ctx", "head", None),
        P("head", None),
        P(),
    )
    out_specs = (
        P("ctx", "head", None),
        P("ctx", "head", None),
        P("ctx", "head", None),
        P("ctx", "head", None),
        P("head", None),
    )
    return jax.shard_map(local, mesh=mesh, in_specs=in_specs, out_specs=out_specs, check_vma=False)
```

profile of v0, /device:TPU:0, one launch (start us, length us, event | category | flops | bytes accessed | tf_op | source)
XLA Modules:
  0.0 321.5 jit_solution(7167898939765990491)
XLA Ops:
  7.3 0.9 convert_reduce_fusion
  8.3 0.8 fusion.16
  9.9 4.3 %copy.122 = bf16[2,512,8,128]{1,3,2,0:T(8,128)(2,1)} copy(bf16[2,512,8,128]{3,2,1,0:T(8,128)(2,1)} %bitcast.69) | data formatting | bytes 4194304 | tf_op jit(solution)/shard_map/reshape | solution.py:62
  15.3 2.4 fusion.4
  17.7 1.5 slice_add_fusion.2
  20.6 0.8 dynamic-update-slice
  21.3 42.4 %all-reduce.2 = f32[16]{0:T(128)S(1)} all-reduce(f32[16]{0:T(128)S(1)} %dynamic-update-slice), channel_id=1, replica_groups=mesh['ctx'=16,'head'=8] {'ctx'}, use_global_device_ids=true, to_apply=%add.2 | all-reduce | flops 16 | bytes 128
  64.5 4.3 %copy.135 = bf16[2,512,8,128]{1,3,2,0:T(8,128)(2,1)} copy(bf16[2,512,8,128]{3,2,1,0:T(8,128)(2,1)} %bitcast.70) | data formatting | bytes 4194304 | tf_op jit(solution)/shard_map/reshape | solution.py:61
  69.9 1.1 copy-done.14
  71.0 2.4 bitcast_convert_fusion
  73.4 0.8 copy-done.10
  74.2 1.4 copy-done.7
  75.6 5.6 %multiply_convert_fusion.1 = bf16[2,8,512,512]{3,2,1,0:T(8,128)(2,1)} fusion(f32[2,512,512]{2,1,0:T(8,128)S(1)} %and_convert_fusion, bf16[2,512,8,128]{1,3,2,0:T(8,128)(2,1)S(1)} %copy-done.4, bf16[2,512,8,128]{1,3,2,0:T(8,128)(2,1)S(1)} %copy-done.7), kind=kOutput, calls=%fused_computation.3 | convolution fusion | flops 1082130432 | bytes 14680064 | tf_op jit(solution)/shard_map/cthd,cshd->chts/dot_general | solution.py:64
  81.2 11.8 %all-gather.3.cloned.1.call-done = f32[16,8,128,128]{3,2,1,0:T(8,128)} async-done(((f32[1,8,128,128]{3,2,1,0:T(8,128)}), f32[16,8,128,128]{3,2,1,0:T(8,128)}) %all-gather.3.cloned.1.call-update) | async-done | bytes 8388624 | tf_op jit(solution)/shard_map/all_gather | solution.py:20
  93.1 2.4 fusion.18
  95.5 7.9 %multiply_reduce_fusion.2 = (f32[2,512]{1,0:T(2,128)S(1)}, f32[2,512,8,128]{3,1,2,0:T(8,128)}) fusion(f32[2,8,128,512]{2,3,1,0:T(8,128)S(1)} %fusion.18, f32[2,512]{1,0:T(2,128)S(1)} %get-tuple-element.160, bf16[2,8,512,512]{3,2,1,0:T(8,128)(2,1)} %multiply_convert_fusion.1, bf16[2,512,8,128]{3,2,1,0:T(8,128)(2,1)S(1)} %bitcast.65), kind=kOutput, calls=%fused_computation.14 | convolution fusion | flops 1077935104 | bytes 18882560 | tf_op jit(solution)/shard_map/chts,cshd->cthd/dot_general | solution.py:68
  103.4 14.4 %psum.21 = f32[2,512]{1,0:T(2,128)S(1)} all-reduce(f32[2,512]{1,0:T(2,128)S(1)} %get-tuple-element.173), channel_id=1, replica_groups=mesh['ctx'=16,'head'=8] {'head'}, use_global_device_ids=true, to_apply=%region_7.8 | all-reduce | flops 1024 | bytes 8192 | tf_op jit(solution)/shard_map/psum | solution.py:97
  117.8 5.0 %multiply_reduce_fusion = (f32[8,128]{1,0:T(8,128)S(1)}, f32[2,512]{1,0:T(2,128)S(1)}) fusion(f32[2,512,8,128]{3,2,1,0:T(8,128)} %bitcast_convert_fusion, f32[2,512,8,128]{3,1,2,0:T(8,128)} %get-tuple-element.174, f32[2,512]{1,0:T(2,128)S(1)} %add_rsqrt_fusion, f32[8,128]{1,0:T(8,128)S(1)} %copy-done.15), kind=kLoop, calls=%fused_computation.9 | loop fusion | flops 6289408 | bytes 8404992 | tf_op jit(solution)/shard_map/reduce_sum | solution.py:105
  122.8 12.6 %psum.22 = f32[2,512]{1,0:T(2,128)S(1)} all-reduce(f32[2,512]{1,0:T(2,128)S(1)} %get-tuple-element.136), channel_id=1, replica_groups=mesh['ctx'=16,'head'=8] {'head'}, use_global_device_ids=true, to_apply=%region_9.10 | all-reduce | flops 1024 | bytes 8192 | tf_op jit(solution)/shard_map/psum | solution.py:97
  135.5 5.5 %subtract_convert_fusion = (bf16[2,512,8,128]{3,1,2,0:T(8,128)(2,1)S(1)}, bf16[2,512,8,128]{3,1,2,0:T(8,128)(2,1)}) fusion(f32[2,512,8,128]{3,1,2,0:T(8,128)} %get-tuple-element.174, f32[2,512,8,128]{3,2,1,0:T(8,128)} %bitcast_convert_fusion, f32[2,512]{1,0:T(2,128)S(1)} %fusion.15, f32[8,128]{1,0:T(8,128)S(1)} %copy-done.15, f32[2,512]{1,0:T(2,128)S(1)} %add_rsqrt_fusion), kind=kLoop, calls=%fused_computation.11 | loop fusion | flops 8388608 | bytes 12595200 | tf_op jit(solution)/shard_map/convert_element_type | solution.py:104
  141.0 0.7 fusion.2
  142.3 1.6 slice_add_fusion
  144.0 0.7 pad_maximum_fusion
  145.1 4.5 %fusion.17 = f32[2,8,128,512]{2,3,1,0:T(8,128)} fusion(bf16[2,512,8,128]{3,1,2,0:T(8,128)(2,1)} %copy-done.2, f32[1,8,128,128]{3,2,1,0:T(8,128)S(1)} %get-tuple-element.164, f32[8,128,128]{2,1,0:T(8,128)S(1)} %get-tuple-element.133, f32[2]{0:T(128)S(1)} %bitcast.76), kind=kOutput, calls=%fused_computation.55 | convolution fusion | flops 269221888 | bytes 7340040 | tf_op jit(solution)/shard_map/cthe,chde->cthd/dot_general | solution.py:120
  149.6 4.2 %multiply_convert_fusion = bf16[2,8,512,512]{3,2,1,0:T(8,128)(2,1)S(1)} fusion(f32[2,512,512]{2,1,0:T(8,128)} %copy-done.10, bf16[2,512,8,128]{3,1,2,0:T(8,128)(2,1)S(1)} %copy-done.3, bf16[2,512,8,128]{3,2,1,0:T(8,128)(2,1)S(1)} %bitcast.67), kind=kOutput, calls=%fused_computation.2 | convolution fusion | flops 1082130432 | bytes 14680064 | tf_op jit(solution)/shard_map/cthe,cshe->chts/dot_general | solution.py:108
  153.8 7.7 %fusion.1 = bf16[2,512,8,128]{3,1,2,0:T(8,128)(2,1)S(1)} fusion(f32[2,8,128,512]{2,3,1,0:T(8,128)} %fusion.17, bf16[2,8,512,512]{3,2,1,0:T(8,128)(2,1)S(1)} %multiply_convert_fusion, bf16[2,512,8,128]{1,3,2,0:T(8,128)(2,1)S(1)} %copy-done.8, f32[2,512]{1,0:T(2,128)S(1)} %get-tuple-element.160), kind=kOutput, calls=%fused_computation.7 | convolution fusion | flops 1076887552 | bytes 16781312 | tf_op jit(solution)/shard_map/chts,cshd->cthd/dot_general | solution.py:111
  161.4 2.7 copy.132
  164.1 2.7 copy.127
  166.8 77.6 %psum.23 = f32[8,128]{1,0:T(8,128)S(1)} all-reduce(f32[8,128]{1,0:T(8,128)S(1)} %get-tuple-element.135), channel_id=1, replica_groups=mesh['ctx'=16,'head'=8] {'ctx'}, use_global_device_ids=true, to_apply=%region_14.15 | all-reduce | flops 1024 | bytes 8192 | tf_op jit(solution)/shard_map/psum | solution.py:106
  245.0 8.5 %fusion.23 = f32[2,8,128,512]{2,3,1,0:T(8,128)} fusion(bf16[2,512,8,128]{3,1,2,0:T(8,128)(2,1)} %copy-done.2, bf16[2,8,512,512]{3,2,1,0:T(8,128)(2,1)} %multiply_convert_fusion.1), kind=kOutput, calls=%fused_computation.61 | convolution fusion | flops 1073741824 | bytes 14680064 | tf_op jit(solution)/shard_map/chts,cthe->cshe/dot_general | solution.py:117
  253.5 39.5 %while.27 = (s32[]{:T(128)}, f32[8,128,128]{2,1,0:T(8,128)S(1)}, s32[]{:T(128)}, f32[16,8,128,128]{3,2,1,0:T(8,128)}, f32[16]{0:T(128)S(1)}, /*index=5*/s32[]{:T(128)}, s32[]{:T(128)}, s32[]{:T(128)}, s32[]{:T(128)}, f32[1]{0:T(128)}) while((s32[]{:T(128)}, f32[8,128,128]{2,1,0:T(8,128)S(1)}, s32[]{:T(128)}, ...), condition=%wide.region_12.13_spmd, body=%wide.region_11.12_spmd.sunk | while | flops 262151 | bytes 1573043 | solution.py:29
  253.6 0.7 dynamic_slice.35
  254.9 1.2 bitcast_add_fusion.8
  256.2 0.7 dynamic_slice.35
  257.6 1.2 bitcast_add_fusion.8
  258.8 0.7 dynamic_slice.35
  260.2 1.2 bitcast_add_fusion.8
  261.5 0.7 dynamic_slice.35
  262.8 1.2 bitcast_add_fusion.8
  264.1 0.7 dynamic_slice.35
  265.5 1.2 bitcast_add_fusion.8
  266.7 0.7 dynamic_slice.35
  268.1 1.2 bitcast_add_fusion.8
  269.4 0.7 dynamic_slice.35
  270.7 1.2 bitcast_add_fusion.8
  272.0 0.7 dynamic_slice.35
  273.4 1.2 bitcast_add_fusion.8
  274.6 0.7 dynamic_slice.35
  276.0 1.2 bitcast_add_fusion.8
  277.3 0.7 dynamic_slice.35
  278.6 1.2 bitcast_add_fusion.8
  279.9 0.7 dynamic_slice.35
  281.3 1.2 bitcast_add_fusion.8
  283.9 1.2 bitcast_add_fusion.8
  285.2 0.7 dynamic_slice.35
  286.5 1.2 bitcast_add_fusion.8
  289.2 1.2 bitcast_add_fusion.8
  291.8 1.2 bitcast_add_fusion.8
  293.1 2.9 fusion.7
  296.0 1.4 copy-done.11
  297.4 1.4 fusion.6
  298.8 2.7 copy.144
  301.5 8.8 %fusion = bf16[2,512,8,128]{3,1,2,0:T(8,128)(2,1)} fusion(f32[2,8,128,512]{2,3,1,0:T(8,128)} %fusion.7, bf16[2,8,512,512]{3,2,1,0:T(8,128)(2,1)} %copy-done.1, bf16[2,512,8,128]{1,3,2,0:T(8,128)(2,1)S(1)} %copy-done.6, f32[2,512]{1,0:T(2,128)S(1)} %get-tuple-element.170), kind=kOutput, calls=%fused_computation.5 | convolution fusion | flops 1076887552 | bytes 16781312 | tf_op jit(solution)/shard_map/chts,cthd->cshd/dot_general | solution.py:114
  310.4 4.3 %copy.138 = bf16[2,512,8,128]{3,2,1,0:T(8,128)(2,1)} copy(bf16[2,512,8,128]{3,1,2,0:T(8,128)(2,1)} %fusion) | data formatting | bytes 4194304 | tf_op jit(solution)/shard_map/convert_element_type | solution.py:142
  (62 shorter events, 7.3 us)
Async XLA Ops:
  7.2 8.2 %copy-start = (bf16[1024,8,128]{2,1,0:T(8,128)(2,1)S(1)}, bf16[1024,8,128]{2,1,0:T(8,128)(2,1)}, u32[]{:S(2)}) copy-start(bf16[1024,8,128]{2,1,0:T(8,128)(2,1)} %param.12) | copy-start | bytes 6291460
  7.2 85.8 %all-gather.3.cloned.1.call-start = ((), (), s32[]{:S(2)}) async-start(), calls=%async_computation | async-start | bytes 8912896 | tf_op jit(solution)/shard_map/all_gather | solution.py:20
  17.7 2.3 copy-start.16
  19.3 234.2 %all-gather.5.cloned.1.call-start = ((), (), s32[]{:S(2)}) async-start(), calls=%async_computation.1 | async-start | bytes 8912896 | tf_op jit(solution)/shard_map/all_gather | solution.py:20
  69.4 1.6 copy-start.14
  71.0 3.2 copy-start.10
  71.0 3.2 copy-start.4
  71.0 4.6 %copy-start.7 = (bf16[2,512,8,128]{1,3,2,0:T(8,128)(2,1)S(1)}, bf16[2,512,8,128]{1,3,2,0:T(8,128)(2,1)}, u32[]{:S(2)}) copy-start(bf16[2,512,8,128]{1,3,2,0:T(8,128)(2,1)} %copy.122) | copy-start | bytes 6291460
  95.5 22.3 %copy-start.15 = (f32[8,128]{1,0:T(8,128)S(1)}, f32[8,128]{1,0:T(8,128)}, u32[]{:S(2)}) copy-start(f32[8,128]{1,0:T(8,128)} %param.14) | copy-start | bytes 12292
  135.5 5.5 %copy-start.5 = (bf16[2,512,8,128]{1,3,2,0:T(8,128)(2,1)S(1)}, bf16[2,512,8,128]{1,3,2,0:T(8,128)(2,1)}, u32[]{:S(2)}) copy-start(bf16[2,512,8,128]{1,3,2,0:T(8,128)(2,1)} %copy.135) | copy-start | bytes 6291460
  141.0 1.4 copy-start.2
  145.1 4.5 %copy-start.3 = (bf16[2,512,8,128]{3,1,2,0:T(8,128)(2,1)S(1)}, bf16[2,512,8,128]{3,1,2,0:T(8,128)(2,1)}, u32[]{:S(2)}) copy-start(bf16[2,512,8,128]{3,1,2,0:T(8,128)(2,1)} %copy-done.2) | copy-start | bytes 6291460
  149.6 4.2 %copy-start.8 = (bf16[2,512,8,128]{1,3,2,0:T(8,128)(2,1)S(1)}, bf16[2,512,8,128]{1,3,2,0:T(8,128)(2,1)}, u32[]{:S(2)}) copy-start(bf16[2,512,8,128]{1,3,2,0:T(8,128)(2,1)} %copy.122) | copy-start | bytes 6291460
  153.8 7.7 %copy-start.1 = (bf16[2,8,512,512]{3,2,1,0:T(8,128)(2,1)}, bf16[2,8,512,512]{3,2,1,0:T(8,128)(2,1)S(1)}, u32[]{:S(2)}) copy-start(bf16[2,8,512,512]{3,2,1,0:T(8,128)(2,1)S(1)} %multiply_convert_fusion) | copy-start | bytes 25165828
  161.4 2.7 copy-start.12
  253.5 39.6 %copy-start.13 = (f32[1,8,128,128]{3,2,1,0:T(8,128)S(1)}, f32[1,8,128,128]{3,2,1,0:T(8,128)}, u32[]{:S(2)}) copy-start(f32[1,8,128,128]{3,2,1,0:T(8,128)} %get-tuple-element.158) | copy-start | bytes 1572868
  293.1 2.9 copy-start.9
  293.1 4.3 %copy-start.11 = (f32[2,8,128,512]{2,3,1,0:T(8,128)S(1)}, f32[2,8,128,512]{2,3,1,0:T(8,128)}, u32[]{:S(2)}) copy-start(f32[2,8,128,512]{2,3,1,0:T(8,128)} %fusion.23) | copy-start | bytes 12582916
  298.8 2.7 copy-start.6
Sparse Core Ops, SparseCore 0:
  19.4 73.6 all-gather.2
  144.1 105.5 all-gather.4
where the time goes:
time: 323 us; the launch traced here: 321 us
  blocking collectives  147 us (46%)
  matrix products  57 us (18%)
  other arithmetic  40 us (12%)
  local copies, waits for them, and re-layouts  38.6 us (12%)
  between operations  16.2 us (5%)
  waiting for transfers between devices  11.9 us (4%)
  loops' own time  10.9 us (3%)
    psum x1, blocking collectives, local(): lax.psum(gain_local, 'ctx') / math.sqrt(shard_rows * shard_count)  77.6 us
    unnamed x1, blocking collectives  42.4 us
    psum x2, blocking collectives, local(): squares, cross_sum = lax.psum((local_squares, local_cross), 'head')  26.9 us
    add x15, other arithmetic, chain_state(): later[0] + (1.0 - later[1]) * earlier[0]  18.7 us
    all_gather x2, waiting for transfers between devices, prefix(): gathered = jax.tree.map(lambda a: lax.all_gather(a, axis), part)  11.8 us
    another operation x2, loops' own time, prefix(): return lax.fori_loop(0, ahead, one, state)  10.9 us
    dynamic_slice x15, local copies, waits for them, and re-layouts, one(): lax.dynamic_index_in_dim(a, source, 0, False)  9.98 us
    dot_general x1, matrix products, local(): jnp.einsum('chts,cthd->cshd', grad_scores, tiled_query, preferred_element...  8.85 us
  transfers between devices with their start and end apart: 2, of which 1 were waited for; matrix products, arithmetic and copies ran while one was open for 15% of the time, Pallas kernels for 0%

commit v1 on v0

v1 whole, which is shorter than its diff:
```python
import functools
import math

import jax
import jax.numpy as jnp
from jax import lax
from jax.experimental import pallas as pl
from jax.experimental.pallas import tpu as pltpu
from jax.sharding import PartitionSpec as P

HEADS = 64
HEAD_DIM = 128
EPSILON = 1e-06
TOKENS = 16384
SHARDS = 16
PEERS = 8
ROWS = 1024
LOCAL = 8
B = 128
TILES = ROWS // B
GROUPS = 2
G = LOCAL // GROUPS
PIECE = HEAD_DIM // SHARDS
MESH = pl.DeviceIdType.MESH
F32 = jnp.float32
BF16 = jnp.bfloat16

OFFSETS = sorted(
    range(1, SHARDS), key=lambda o: -(min(o // 4, 4 - o // 4) + min(o % 4, 4 - o % 4))
)


def nn(a, b):
    return lax.dot_general(a, b, (((1,), (0,)), ((), ())), preferred_element_type=F32)


def nt(a, b):
    return lax.dot_general(a, b, (((1,), (1,)), ((), ())), preferred_element_type=F32)


def tn(a, b):
    return lax.dot_general(a, b, (((0,), (0,)), ((), ())), preferred_element_type=F32)


def loop(count, body):
    def step(i, carry):
        body(i)
        return carry

    lax.fori_loop(0, count, step, 0)


def kernel(
    q_hbm, k_hbm, v_hbm, u_hbm, gain_ref, starts_ref,
    n_out, dq_out, dk_out, dv_out, dgain_ref,
    q_raw, k_raw, v_raw, u_raw,
    qh, kh, vh, uh, gh, ah, ath, bth, tmp, att, lbuf, rbuf,
    sqa, cra, invb, cob, gpart,
    st, rx, px, inc, st2, rx2, px2, inc2,
    stat_rx, stat_tx, gain_rx, gain_tx,
    kc_sm, mp_sm, nz_sm, keep_sm,
    in_sem, out_sem, s1, r1, s2, r2, s3, r3, s4, r4, hs, hr, gs, gr_sem,
):
    me = lax.axis_index("ctx")
    my_head = lax.axis_index("head")
    y, z = me // 4, lax.rem(me, 4)

    def at_offset(o):
        return lax.rem(y + o // 4, 4) * 4 + lax.rem(z + o % 4, 4)

    hbm_in = (k_hbm, v_hbm, q_hbm, u_hbm)
    raw_in = (k_raw, v_raw, q_raw, u_raw)

    def load(a, c):
        rows = pl.ds(c * B, B)
        return pltpu.make_async_copy(hbm_in[a].at[rows], raw_in[a].at[rows], in_sem.at[a, c])

    for c in range(TILES):
        load(0, c).start()
        load(1, c).start()
    for c in range(TILES):
        load(2, c).start()
        load(3, c).start()

    barrier = pltpu.get_barrier_semaphore()
    for k in range(1, SHARDS):
        pl.semaphore_signal(
            barrier, inc=1, device_id={"ctx": lax.rem(me + k, SHARDS)}, device_id_type=MESH
        )
    for k in range(1, PEERS):
        pl.semaphore_signal(
            barrier, inc=1, device_id={"head": lax.rem(my_head + k, PEERS)}, device_id_type=MESH
        )

    docs = starts_ref.shape[0]

    def opens(position, width):
        found = jnp.int32(0)
        for d in range(docs):
            found = found + (starts_ref[d] // width == position).astype(jnp.int32)
        return 1.0 - jnp.minimum(found, 1).astype(F32)

    running = jnp.float32(1.0)
    for c in range(TILES):
        flag = opens(me * TILES + c, B)
        running = running * flag
        kc_sm[c] = flag
        mp_sm[c] = running
    running = jnp.float32(1.0)
    for c in reversed(range(TILES)):
        nz_sm[c] = running
        running = running * kc_sm[c]

    def shard_flag(i):
        keep_sm[i] = opens(i, ROWS)

    loop(SHARDS, shard_flag)

    row = lax.broadcasted_iota(jnp.int32, (B, B), 0)
    col = lax.broadcasted_iota(jnp.int32, (B, B), 1)

    def lower(x):
        return jnp.where(row >= col, x, 0.0).astype(BF16)

    def upper(x):
        return jnp.where(row <= col, x, 0.0).astype(BF16)

    def unpack(raw, out, c):
        out[:, c] = jnp.swapaxes(raw[pl.ds(pl.multiple_of(c * B, B), B)], 0, 1)

    def states(g):
        heads = range(g * G, (g + 1) * G)

        def body(c):
            flag = kc_sm[c]
            for h in heads:
                part = tn(kh[h, c], vh[h, c])
                kept = flag * st[h].reshape(B, B)
                lbuf[h, c] = kept
                st[h] = (part + kept).reshape(SHARDS, PIECE, B)

        loop(TILES, body)

    def group(g):
        return pl.ds(g * G, G)

    def scatter(src, dst, ssem, rsem, g):
        for n, o in enumerate(OFFSETS):
            p = at_offset(o)
            pltpu.make_async_remote_copy(
                src.at[group(g), p], dst.at[me, group(g)], ssem.at[g, n], rsem.at[g, me],
                device_id={"ctx": p}, device_id_type=MESH,
            ).start()
        dst[me, group(g)] = src[group(g), me]

    def scatter_done(src, dst, ssem, rsem, g):
        for n, o in enumerate(OFFSETS):
            p = at_offset(o)
            pltpu.make_async_remote_copy(
                src.at[group(g), p], dst.at[me, group(g)], ssem.at[g, n], rsem.at[g, me],
                device_id={"ctx": p}, device_id_type=MESH,
            ).wait_send()

    def back(px, inc, ssem, rsem, g, i):
        return pltpu.make_async_remote_copy(
            px.at[i, group(g)], inc.at[me, group(g)], ssem.at[g, i], rsem.at[g, me],
            device_id={"ctx": i}, device_id_type=MESH,
        )

    def chain(src, rx, px, inc, s_in, r_in, s_out, r_out, g, forward):
        first = 0 if forward else SHARDS - 1
        px[first, group(g)] = jnp.zeros((G, PIECE, B), F32)

        def step(turn, total):
            i = turn if forward else SHARDS - 1 - turn

            @pl.when(i != me)
            def _():
                pltpu.make_async_remote_copy(
                    src.at[group(g), i], rx.at[i, group(g)], s_in.at[g, 0], r_in.at[g, i],
                    device_id={"ctx": i}, device_id_type=MESH,
                ).wait_recv()

            total = rx[i, group(g)] + keep_sm[i] * total

            @pl.when(turn < SHARDS - 1)
            def _():
                px[i + 1 if forward else i - 1, group(g)] = total

            @pl.when(i != me)
            def _():
                back(px, inc, s_out, r_out, g, i).start()

            return total

        lax.fori_loop(0, SHARDS, step, jnp.zeros((G, PIECE, B), F32))
        inc[me, group(g)] = px[me, group(g)]

    def arrived(px, inc, ssem, rsem, g):
        for o in OFFSETS:
            p = at_offset(o)
            pltpu.make_async_remote_copy(
                px.at[p, group(g)], inc.at[p, group(g)], ssem.at[g, p], rsem.at[g, p],
                device_id={"ctx": p}, device_id_type=MESH,
            ).wait_recv()

    def back_done(px, inc, ssem, rsem, g):
        for o in OFFSETS:
            back(px, inc, ssem, rsem, g, at_offset(o)).wait_send()

    st[...] = jnp.zeros_like(st)

    def first_load(c):
        load(0, c).wait()
        load(1, c).wait()
        unpack(k_raw, kh, c)
        unpack(v_raw, vh, c)

    loop(TILES, first_load)
    states(0)
    pl.semaphore_wait(barrier, SHARDS - 1 + PEERS - 1)
    scatter(st, rx, s1, r1, 0)
    for g in range(1, GROUPS):
        states(g)
        scatter(st, rx, s1, r1, g)

    def second_load(c):
        load(2, c).wait()
        load(3, c).wait()
        unpack(q_raw, qh, c)
        unpack(u_raw, uh, c)

    loop(TILES, second_load)

    def scores(g):
        def body(c):
            for h in range(g * G, (g + 1) * G):
                ah[h, c] = lower(nt(qh[h, c], kh[h, c]))

        loop(TILES, body)

    def scores_t(g):
        def body(c):
            for h in range(g * G, (g + 1) * G):
                ath[h, c] = upper(nt(kh[h, c], qh[h, c]))

        loop(TILES, body)

    scores(0)
    for g in range(GROUPS):
        chain(st, rx, px, inc, s1, r1, s2, r2, g, True)
        if g + 1 < GROUPS:
            scores(g + 1)
    for g in range(GROUPS):
        scores_t(g)

    for g in range(GROUPS):
        arrived(px, inc, s2, r2, g)

        def body(c, g=g):
            sq = jnp.zeros((B, B), F32) if g == 0 else sqa[c]
            cr = jnp.zeros((B, B), F32) if g == 0 else cra[c]
            reach = mp_sm[c]
            for h in range(g * G, (g + 1) * G):
                entry = (lbuf[h, c] + reach * inc[:, h].reshape(B, B)).astype(BF16)
                rbuf[h, c] = entry
                out = nn(
                    jnp.concatenate([ah[h, c], qh[h, c]], axis=1),
                    jnp.concatenate([vh[h, c], entry], axis=0),
                )
                att[h, c] = out
                sq = sq + out * out
                cr = cr + uh[h, c].astype(F32) * gain_ref[h : h + 1, :] * out
            sqa[c] = sq
            cra[c] = cr

        loop(TILES, body)

    sq_cols = jnp.zeros((B, B), F32)
    cr_cols = jnp.zeros((B, B), F32)
    for c in range(TILES):
        sq_cols = jnp.where(col == c, jnp.sum(sqa[c], axis=1, keepdims=True), sq_cols)
        cr_cols = jnp.where(col == c, jnp.sum(cra[c], axis=1, keepdims=True), cr_cols)
    stat_tx[0] = jnp.transpose(sq_cols)[:TILES]
    stat_tx[1] = jnp.transpose(cr_cols)[:TILES]

    def tell(k):
        to = lax.rem(my_head + k, PEERS)
        return pltpu.make_async_remote_copy(
            stat_tx, stat_rx.at[my_head], hs.at[k], hr.at[my_head],
            device_id={"head": to}, device_id_type=MESH,
        )

    for k in range(1, PEERS):
        tell(k).start()
    stat_rx[my_head] = stat_tx[...]
    for k in range(1, PEERS):
        source = lax.rem(my_head + k, PEERS)
        pltpu.make_async_remote_copy(
            stat_tx, stat_rx.at[source], hs.at[k], hr.at[source],
            device_id={"head": source}, device_id_type=MESH,
        ).wait_recv()
    sums = stat_rx[0]
    for k in range(1, PEERS):
        sums = sums + stat_rx[k]
    features = HEADS * HEAD_DIM
    inverse = 1.0 / jnp.sqrt(sums[0] / features + EPSILON)
    pull = inverse * inverse * inverse * sums[1] / features
    inv_cols = jnp.transpose(jnp.concatenate([inverse] * (B // TILES), axis=0))
    pull_cols = jnp.transpose(jnp.concatenate([pull] * (B // TILES), axis=0))
    for c in range(TILES):
        invb[c] = jnp.broadcast_to(inv_cols[:, c : c + 1], (B, B))
        cob[c] = jnp.broadcast_to(pull_cols[:, c : c + 1], (B, B))

    gpart[...] = jnp.zeros_like(gpart)
    st2[...] = jnp.zeros_like(st2)
    for g in range(GROUPS):

        def body(turn, g=g):
            c = TILES - 1 - turn
            flag = kc_sm[c]
            inv = invb[c]
            co = cob[c]
            for h in range(g * G, (g + 1) * G):
                gain = gain_ref[h : h + 1, :]
                out = att[h, c]
                up = uh[h, c].astype(F32)
                scaled = out * inv
                ah[h, c] = (scaled * gain).astype(BF16)
                grad = (inv * (up * gain) - out * co).astype(BF16)
                gh[h, c] = grad
                gpart[h] += jnp.sum((up * scaled).reshape(B // 8, 8, B), axis=0)
                later = st2[h].reshape(B, B)
                lbuf[h, c] = later
                st2[h] = (flag * (tn(qh[h, c], grad) + later)).reshape(SHARDS, PIECE, B)

        loop(TILES, body)
        scatter(st2, rx2, s3, r3, g)

    for h in range(LOCAL):
        gain_tx[h : h + 1, :] = jnp.sum(gpart[h], axis=0, keepdims=True)

    def tell_gain(k):
        to = lax.rem(me + k, SHARDS)
        return pltpu.make_async_remote_copy(
            gain_tx, gain_rx.at[me], gs.at[k], gr_sem.at[me],
            device_id={"ctx": to}, device_id_type=MESH,
        )

    for k in range(1, SHARDS):
        tell_gain(k).start()
    gain_rx[me] = gain_tx[...]

    def store(stage, out, a, c):
        rows = pl.ds(c * B, B)
        return pltpu.make_async_copy(stage.at[rows], out.at[rows], out_sem.at[a, c])

    def pack(value, stage, out, a, c):
        stage[pl.ds(pl.multiple_of(c * B, B), B)] = jnp.swapaxes(value, 0, 1)
        store(stage, out, a, c).start()

    def grad_q(g):
        def body(c):
            for h in range(g * G, (g + 1) * G):
                grad = gh[h, c]
                b = lower(nt(grad, vh[h, c]))
                bth[h, c] = upper(nt(vh[h, c], grad))
                rbuf[h, c] = (nn(b, kh[h, c]) + nt(grad, rbuf[h, c])).astype(BF16)

        loop(TILES, body)

    def put_normed(c):
        pack(ah[:, c], q_raw, n_out, 0, c)

    loop(TILES, put_normed)
    for g in range(GROUPS):
        grad_q(g)
        chain(st2, rx2, px2, inc2, s3, r3, s4, r4, g, False)

    def put_dq(c):
        pack(rbuf[:, c], u_raw, dq_out, 1, c)

    loop(TILES, put_dq)

    for k in range(1, SHARDS):
        source = lax.rem(me + k, SHARDS)
        pltpu.make_async_remote_copy(
            gain_tx, gain_rx.at[source], gs.at[k], gr_sem.at[source],
            device_id={"ctx": source}, device_id_type=MESH,
        ).wait_recv()
    total = gain_rx[0]
    for k in range(1, SHARDS):
        total = total + gain_rx[k]
    dgain_ref[...] = total / math.sqrt(TOKENS)

    for g in range(GROUPS):
        arrived(px2, inc2, s4, r4, g)

        def body(c, g=g):
            reach = nz_sm[c]
            for h in range(g * G, (g + 1) * G):
                leave = (lbuf[h, c] + reach * inc2[:, h].reshape(B, B)).astype(BF16)
                dk = nn(bth[h, c], qh[h, c]) + nt(vh[h, c], leave)
                dv = nn(
                    jnp.concatenate([ath[h, c], kh[h, c]], axis=1),
                    jnp.concatenate([gh[h, c], leave], axis=0),
                )
                ah[h, c] = dk.astype(BF16)
                uh[h, c] = dv.astype(BF16)
            if g == GROUPS - 1:
                pack(ah[:, c], k_raw, dk_out, 2, c)
                pack(uh[:, c], v_raw, dv_out, 3, c)

        loop(TILES, body)

    for g in range(GROUPS):
        scatter_done(st, rx, s1, r1, g)
        back_done(px, inc, s2, r2, g)
        scatter_done(st2, rx2, s3, r3, g)
        back_done(px2, inc2, s4, r4, g)
    for k in range(1, PEERS):
        tell(k).wait_send()
    for k in range(1, SHARDS):
        tell_gain(k).wait_send()

    def drain(c):
        store(q_raw, n_out, 0, c).wait()
        store(u_raw, dq_out, 1, c).wait()
        store(k_raw, dk_out, 2, c).wait()
        store(v_raw, dv_out, 3, c).wait()

    loop(TILES, drain)


def local(queries, key_rows, value_rows, grad_normed, norm_gain, document_starts):
    anywhere = pl.BlockSpec(memory_space=pl.ANY)
    vmem = pl.BlockSpec(memory_space=pltpu.VMEM)
    tiles = (LOCAL, TILES, B, B)
    raw = pltpu.VMEM((ROWS, LOCAL, HEAD_DIM), BF16)
    narrow = pltpu.VMEM(tiles, BF16)
    wide = pltpu.VMEM(tiles, F32)
    stats = pltpu.VMEM((TILES, B, B), F32)
    state = pltpu.VMEM((LOCAL, SHARDS, PIECE, B), F32)
    pieces = pltpu.VMEM((SHARDS, LOCAL, PIECE, B), F32)
    dma = pltpu.SemaphoreType.DMA
    big = jax.ShapeDtypeStruct((ROWS, LOCAL, HEAD_DIM), BF16)
    return pl.pallas_call(
        kernel,
        out_shape=(big, big, big, big, jax.ShapeDtypeStruct((LOCAL, HEAD_DIM), F32)),
        in_specs=[anywhere] * 4 + [vmem, pl.BlockSpec(memory_space=pltpu.SMEM)],
        out_specs=(anywhere,) * 4 + (vmem,),
        scratch_shapes=[raw] * 4
        + [narrow] * 8
        + [pltpu.VMEM((8, 128), F32), wide, wide, narrow]
        + [stats] * 4
        + [pltpu.VMEM((LOCAL, 8, B), F32)]
        + [state, pieces, pieces, pieces, state, pieces, pieces, pieces]
        + [
            pltpu.VMEM((PEERS, 2, TILES, B), F32),
            pltpu.VMEM((2, TILES, B), F32),
            pltpu.VMEM((SHARDS, LOCAL, B), F32),
            pltpu.VMEM((LOCAL, B), F32),
        ]
        + [pltpu.SMEM((TILES,), F32)] * 3
        + [pltpu.SMEM((SHARDS,), F32)]
        + [dma((4, TILES)), dma((4, TILES))]
        + [dma((GROUPS, SHARDS))] * 8
        + [dma((PEERS,))] * 2
        + [dma((SHARDS,))] * 2,
        compiler_params=pltpu.CompilerParams(
            collective_id=0, has_side_effects=True, vmem_limit_bytes=67043328
        ),
    )(queries, key_rows, value_rows, grad_normed, norm_gain, document_starts)


def solution(mesh):
    rows = P("ctx", "head", None)
    return jax.shard_map(
        local,
        mesh=mesh,
        in_specs=(rows, rows, rows, rows, P("head", None), P()),
        out_specs=(rows, rows, rows, rows, P("head", None)),
        check_vma=False,
    )
```

time: 323 us -> 74 us (0.23)
  blocking collectives: 147 us -> 0 us
  Pallas kernels: 0 us -> 62.8 us
  matrix products: 57 us -> 0 us
  other arithmetic: 40 us -> 0 us
  local copies, waits for them, and re-layouts: 38.6 us -> 9.81 us
  between operations: 16.2 us -> 0.65 us
  waiting for transfers between devices: 11.9 us -> 0 us
  loops' own time: 10.9 us -> 0 us
    psum x3 -> x0, blocking collectives: 105 us -> none  [the longest x1 77.6 us: local(): lax.psum(gain_local, 'ctx') / math.sqrt(shard_rows * shard_count)]
    pallas_call x0 -> x1, Pallas kernels: none -> 62.8 us  [local(): pl.pallas_call(kernel, out_shape=(big, big, big, big, jax.ShapeDtypeStruc...]
    dot_general x12 -> x0, matrix products: 57 us -> none  [the longest x1 8.85 us: local(): jnp.einsum('chts,cthd->cshd', grad_scores, tiled_query, preferred_element...]
    unnamed x1 -> x0, blocking collectives: 42.4 us -> none
    add x18 -> x0, other arithmetic: 21.9 us -> none  [the longest x15 18.7 us: chain_state(): later[0] + (1.0 - later[1]) * earlier[0]]
    convert_element_type x4 -> x0, local copies, waits for them, and re-layouts: 12.3 us -> none  [the longest x1 4.26 us: local(): grad_keys = (key_intra + leave_col * key_inter).astype(jnp.bfloat16)]
    all_gather x2 -> x0, waiting for transfers between devices: 11.8 us -> none  [prefix(): gathered = jax.tree.map(lambda a: lax.all_gather(a, axis), part)]
    another operation x2 -> x0, loops' own time: 10.9 us -> none  [prefix(): return lax.fori_loop(0, ahead, one, state)]
  transfers between devices with their start and end apart: 2 -> 0, of which waited for: 1 -> 0; matrix products, arithmetic and copies ran while one was open for 15% -> 0% of each run, Pallas kernels for 0% -> 0%
where the time goes in v1:
time: 74 us; the launch traced here: 73.3 us
  Pallas kernels  62.8 us (85%)
  local copies, waits for them, and re-layouts  9.81 us (13%)
    pallas_call x1, Pallas kernels, local(): pl.pallas_call(kernel, out_shape=(big, big, big, big, jax.ShapeDtypeStruc...  62.8 us
    unnamed x13, local copies, waits for them, and re-layouts  9.81 us

profile of v1, /device:TPU:0, one launch (start us, length us, event | category | flops | bytes accessed | tf_op | source)
XLA Modules:
  0.0 73.3 jit_solution(14608386381253689214)
XLA Ops:
  0.6 62.8 %shard_map.101 = (bf16[1024,8,128]{2,1,0:T(8,128)(2,1)}, bf16[1024,8,128]{2,1,0:T(8,128)(2,1)}, bf16[1024,8,128]{2,1,0:T(8,128)(2,1)}, bf16[1024,8,128]{2,1,0:T(8,128)(2,1)}, f32[8,128]{1,0:T(8,128)}) custom-call(bf16[1024,8,128]{2,1,0:T(8,128)(2,1)} %q_hbm.1, bf16[1024,8,128]{2,1,0:T(8,128)(2,1)} %k_hbm.1, bf16[1024,8,128]{2,1,0:T(8,128)(2,1)} %v_hbm.1, ...), custom_call_target="tpu_custom_call" | custom-call | tf_op jit(solution)/shard_map/pallas_call | solution.py:447
  63.5 0.0 copy-start.2
  63.5 3.2 %copy.16 = bf16[1024,8,128]{2,1,0:T(8,128)(2,1)} copy(bf16[1024,8,128]{2,1,0:T(8,128)(2,1)} %get-tuple-element.10) | data formatting | bytes 4194304
  66.7 0.0 copy-done.2
  66.7 0.0 copy-start.1
  66.7 1.3 %copy.17 = bf16[1024,8,128]{2,1,0:T(8,128)(2,1)} copy(bf16[1024,8,128]{2,1,0:T(8,128)(2,1)S(1)} %copy-done.2) | data formatting | bytes 4194304
  68.0 1.0 %copy-done.1 = bf16[1024,8,128]{2,1,0:T(8,128)(2,1)S(1)} copy-done((bf16[1024,8,128]{2,1,0:T(8,128)(2,1)S(1)}, bf16[1024,8,128]{2,1,0:T(8,128)(2,1)}, u32[]{:S(2)}) %copy-start.1) | copy-done | bytes 2097176
  69.0 0.0 copy-start
  69.0 1.3 %copy.18 = bf16[1024,8,128]{2,1,0:T(8,128)(2,1)} copy(bf16[1024,8,128]{2,1,0:T(8,128)(2,1)S(1)} %copy-done.1) | data formatting | bytes 4194304
  70.3 1.0 %copy-done = bf16[1024,8,128]{2,1,0:T(8,128)(2,1)S(1)} copy-done((bf16[1024,8,128]{2,1,0:T(8,128)(2,1)S(1)}, bf16[1024,8,128]{2,1,0:T(8,128)(2,1)}, u32[]{:S(2)}) %copy-start) | copy-done | bytes 2097176
  71.4 0.0 copy-start.3
  71.4 1.3 %copy.19 = bf16[1024,8,128]{2,1,0:T(8,128)(2,1)} copy(bf16[1024,8,128]{2,1,0:T(8,128)(2,1)S(1)} %copy-done) | data formatting | bytes 4194304
  72.7 0.0 copy-done.3
  72.7 0.6 copy.20
Async XLA Ops:
  63.5 3.2 %copy-start.2 = (bf16[1024,8,128]{2,1,0:T(8,128)(2,1)S(1)}, bf16[1024,8,128]{2,1,0:T(8,128)(2,1)}, u32[]{:S(2)}) copy-start(bf16[1024,8,128]{2,1,0:T(8,128)(2,1)} %get-tuple-element.11) | copy-start | bytes 6291460
  66.7 2.3 %copy-start.1 = (bf16[1024,8,128]{2,1,0:T(8,128)(2,1)S(1)}, bf16[1024,8,128]{2,1,0:T(8,128)(2,1)}, u32[]{:S(2)}) copy-start(bf16[1024,8,128]{2,1,0:T(8,128)(2,1)} %get-tuple-element.12) | copy-start | bytes 6291460
  69.0 2.3 %copy-start = (bf16[1024,8,128]{2,1,0:T(8,128)(2,1)S(1)}, bf16[1024,8,128]{2,1,0:T(8,128)(2,1)}, u32[]{:S(2)}) copy-start(bf16[1024,8,128]{2,1,0:T(8,128)(2,1)} %get-tuple-element.13) | copy-start | bytes 6291460
  71.4 1.3 %copy-start.3 = (f32[8,128]{1,0:T(8,128)S(1)}, f32[8,128]{1,0:T(8,128)}, u32[]{:S(2)}) copy-start(f32[8,128]{1,0:T(8,128)} %get-tuple-element.14) | copy-start | bytes 12292

commit v2 on v1

v2 whole, which is shorter than its diff:
```python
import functools
import math

import jax
import jax.numpy as jnp
from jax import lax
from jax.experimental import pallas as pl
from jax.experimental.pallas import tpu as pltpu
from jax.sharding import PartitionSpec as P

HEADS = 64
HEAD_DIM = 128
EPSILON = 1e-06
TOKENS = 16384
SHARDS = 16
PEERS = 8
ROWS = 1024
LOCAL = 8
B = 128
TILES = ROWS // B
HALF = ROWS // 2
STEP = 4
PAIR = 2
LIMIT = 32 << 20
LIMIT2 = 12 << 20
GROUPS = 2
G = LOCAL // GROUPS
PIECE = HEAD_DIM // SHARDS
MESH = pl.DeviceIdType.MESH
F32 = jnp.float32
BF16 = jnp.bfloat16

OFFSETS = sorted(
    range(1, SHARDS), key=lambda o: -(min(o // 4, 4 - o // 4) + min(o % 4, 4 - o % 4))
)


def nn(a, b):
    return lax.dot_general(a, b, (((1,), (0,)), ((), ())), preferred_element_type=F32)


def nt(a, b):
    return lax.dot_general(a, b, (((1,), (1,)), ((), ())), preferred_element_type=F32)


def tn(a, b):
    return lax.dot_general(a, b, (((0,), (0,)), ((), ())), preferred_element_type=F32)


def turn(a):
    return jnp.transpose(a)


def loop(count, body):
    def step(i, carry):
        body(i)
        return carry

    lax.fori_loop(0, count, step, 0)


def flags(starts_ref):
    def opens(position, width):
        found = jnp.int32(0)
        for d in range(starts_ref.shape[0]):
            found = found + (starts_ref[d] // width == position).astype(jnp.int32)
        return 1.0 - jnp.minimum(found, 1).astype(F32)

    return opens


def kernel(
    q_hbm, k_hbm, v_hbm, u_hbm, gain_hbm, starts_hbm,
    n_tok, dq_tok, qh, kh, vh, gh, ath, bth, lbuf, inc2, reach_ref, dgain_ref,
    gain_ref, starts_ref, q_raw, k_raw, v_raw, u_raw,
    uh, ah, att, rbuf,
    sqa, cra, invb, cob, gpart,
    st, rx, px, inc, st2, rx2, px2,
    stat_rx, stat_tx, gain_rx, gain_tx,
    kc_sm, mp_sm, keep_sm,
    small_sem, in_sem, s1, r1, s2, r2, s3, r3, s4, r4, hs, hr, gs, gr_sem,
):
    me = lax.axis_index("ctx")
    my_head = lax.axis_index("head")
    y, z = me // 4, lax.rem(me, 4)

    def at_offset(o):
        return lax.rem(y + o // 4, 4) * 4 + lax.rem(z + o % 4, 4)

    hbm_in = (k_hbm, v_hbm, q_hbm, u_hbm)
    raw_in = (k_raw, v_raw, q_raw, u_raw)

    def load(a, c):
        rows = pl.ds(c * HALF, HALF)
        return pltpu.make_async_copy(hbm_in[a].at[rows], raw_in[a].at[rows], in_sem.at[a, c])

    small = [
        pltpu.make_async_copy(starts_hbm, starts_ref, small_sem.at[0]),
        pltpu.make_async_copy(gain_hbm, gain_ref, small_sem.at[1]),
    ]
    for copy in small:
        copy.start()
    for a, b in ((0, 1), (2, 3)):
        for c in range(2):
            load(a, c).start()
            load(b, c).start()

    barrier = pltpu.get_barrier_semaphore()
    for k in range(1, SHARDS):
        pl.semaphore_signal(
            barrier, inc=1, device_id={"ctx": lax.rem(me + k, SHARDS)}, device_id_type=MESH
        )
    for k in range(1, PEERS):
        pl.semaphore_signal(
            barrier, inc=1, device_id={"head": lax.rem(my_head + k, PEERS)}, device_id_type=MESH
        )

    for copy in small:
        copy.wait()
    opens = flags(starts_ref)
    running = jnp.float32(1.0)
    for c in range(TILES):
        flag = opens(me * TILES + c, B)
        running = running * flag
        kc_sm[c] = flag
        mp_sm[c] = running
    running = jnp.float32(1.0)
    for c in reversed(range(TILES)):
        reach_ref[c : c + 1, :] = jnp.full((1, B), running, F32)
        running = running * kc_sm[c]

    def shard_flag(i):
        keep_sm[i] = opens(i, ROWS)

    loop(SHARDS, shard_flag)

    row = lax.broadcasted_iota(jnp.int32, (B, B), 0)
    col = lax.broadcasted_iota(jnp.int32, (B, B), 1)

    def lower(x):
        return jnp.where(row >= col, x, 0.0).astype(BF16)

    def upper(x):
        return jnp.where(row <= col, x, 0.0).astype(BF16)

    def unpack(raw, out, c):
        out[:, c] = jnp.swapaxes(raw[pl.ds(pl.multiple_of(c * B, B), B)], 0, 1)

    def states(g):
        heads = range(g * G, (g + 1) * G)

        def body(i):
            for h in heads:
                total = st[h].reshape(B, B)
                for n in range(STEP):
                    c = i * STEP + n
                    kept = kc_sm[c] * total
                    lbuf[h, c] = kept
                    total = tn(kh[h, c], vh[h, c]) + kept
                st[h] = total.reshape(SHARDS, PIECE, B)

        loop(TILES // STEP, body)

    def group(g):
        return pl.ds(g * G, G)

    def scatter(src, dst, ssem, rsem, g):
        for o in OFFSETS:
            p = at_offset(o)
            pltpu.make_async_remote_copy(
                src.at[group(g), p], dst.at[me, group(g)], ssem.at[0], rsem.at[g],
                device_id={"ctx": p}, device_id_type=MESH,
            ).start()
        dst[me, group(g)] = src[group(g), me]

    def chain(rx, px, inc, r_in, s_out, r_out, g, forward):
        arrived(rx, r_in, g)
        first = 0 if forward else SHARDS - 1
        px[first, group(g)] = jnp.zeros((G, PIECE, B), F32)

        def step(turn, total):
            i = turn if forward else SHARDS - 1 - turn
            total = rx[i, group(g)] + keep_sm[i] * total

            @pl.when(turn < SHARDS - 1)
            def _():
                px[i + 1 if forward else i - 1, group(g)] = total

            @pl.when(i != me)
            def _():
                pltpu.make_async_remote_copy(
                    px.at[i, group(g)], inc.at[me, group(g)], s_out.at[0], r_out.at[g],
                    device_id={"ctx": i}, device_id_type=MESH,
                ).start()

            return total

        lax.fori_loop(0, SHARDS, step, jnp.zeros((G, PIECE, B), F32))
        inc[me, group(g)] = px[me, group(g)]

    def arrived(dst, rsem, g):
        part = dst.at[pl.ds(0, SHARDS - 1), group(g)]
        pltpu.make_async_copy(part, part, rsem.at[g]).wait()

    def sent(buffer, ssem):
        part = buffer.at[pl.ds(0, SHARDS - 1)]
        pltpu.make_async_copy(part, part, ssem.at[0]).wait()

    st[...] = jnp.zeros_like(st)

    def unpack_half(raw, out, half):
        def body(c):
            unpack(raw, out, half * (TILES // 2) + c)

        loop(TILES // 2, body)

    for half in range(2):
        load(0, half).wait()
        unpack_half(k_raw, kh, half)
        load(1, half).wait()
        unpack_half(v_raw, vh, half)

    states(0)
    pl.semaphore_wait(barrier, SHARDS - 1 + PEERS - 1)
    scatter(st, rx, s1, r1, 0)
    for g in range(1, GROUPS):
        states(g)
        scatter(st, rx, s1, r1, g)

    for half in range(2):
        load(2, half).wait()
        unpack_half(q_raw, qh, half)
        load(3, half).wait()
        unpack_half(u_raw, uh, half)

    def scores(g):
        def body(i):
            for n in range(STEP):
                c = i * STEP + n
                for h in range(g * G, (g + 1) * G):
                    a = lower(nt(qh[h, c], kh[h, c]))
                    ah[h, c] = a
                    ath[h, c] = turn(a)

        loop(TILES // STEP, body)

    scores(0)
    for g in range(GROUPS):
        chain(rx, px, inc, r1, s2, r2, g, True)
        if g + 1 < GROUPS:
            scores(g + 1)

    for g in range(GROUPS):
        arrived(inc, r2, g)

        def body(i, g=g):
            for n in range(STEP):
                c = i * STEP + n
                sq = jnp.zeros((B, B), F32) if g == 0 else sqa[c]
                cr = jnp.zeros((B, B), F32) if g == 0 else cra[c]
                reach = mp_sm[c]
                for h in range(g * G, (g + 1) * G):
                    entry = (lbuf[h, c] + reach * inc[:, h].reshape(B, B)).astype(BF16)
                    rbuf[h, c] = entry
                    out = nn(
                        jnp.concatenate([ah[h, c], qh[h, c]], axis=1),
                        jnp.concatenate([vh[h, c], entry], axis=0),
                    )
                    att[h, c] = out
                    sq = sq + out * out
                    cr = cr + uh[h, c].astype(F32) * gain_ref[h : h + 1, :] * out
                sqa[c] = sq
                cra[c] = cr

        loop(TILES // STEP, body)

    sq_cols = jnp.zeros((B, B), F32)
    cr_cols = jnp.zeros((B, B), F32)
    for c in range(TILES):
        sq_cols = jnp.where(col == c, jnp.sum(sqa[c], axis=1, keepdims=True), sq_cols)
        cr_cols = jnp.where(col == c, jnp.sum(cra[c], axis=1, keepdims=True), cr_cols)
    stat_tx[0] = jnp.transpose(sq_cols)[:TILES]
    stat_tx[1] = jnp.transpose(cr_cols)[:TILES]

    for k in range(1, PEERS):
        pltpu.make_async_remote_copy(
            stat_tx, stat_rx.at[my_head], hs.at[0], hr.at[0],
            device_id={"head": lax.rem(my_head + k, PEERS)}, device_id_type=MESH,
        ).start()
    stat_rx[my_head] = stat_tx[...]
    others = stat_rx.at[pl.ds(0, PEERS - 1)]
    pltpu.make_async_copy(others, others, hr.at[0]).wait()
    sums = stat_rx[0]
    for k in range(1, PEERS):
        sums = sums + stat_rx[k]
    features = HEADS * HEAD_DIM
    inverse = 1.0 / jnp.sqrt(sums[0] / features + EPSILON)
    pull = inverse * inverse * inverse * sums[1] / features
    inv_cols = jnp.transpose(jnp.concatenate([inverse] * (B // TILES), axis=0))
    pull_cols = jnp.transpose(jnp.concatenate([pull] * (B // TILES), axis=0))
    for c in range(TILES):
        invb[c] = jnp.broadcast_to(inv_cols[:, c : c + 1], (B, B))
        cob[c] = jnp.broadcast_to(pull_cols[:, c : c + 1], (B, B))

    gpart[...] = jnp.zeros_like(gpart)
    st2[...] = jnp.zeros_like(st2)
    for g in range(GROUPS):

        def body(i, g=g):
            for h in range(g * G, (g + 1) * G):
                gain = gain_ref[h : h + 1, :]
                later = st2[h].reshape(B, B)
                gains = gpart[h]
                for n in range(STEP):
                    c = TILES - 1 - (i * STEP + n)
                    inv = invb[c]
                    out = att[h, c]
                    up = uh[h, c].astype(F32)
                    scaled = out * inv
                    ah[h, c] = (scaled * gain).astype(BF16)
                    grad = (inv * (up * gain) - out * cob[c]).astype(BF16)
                    gh[h, c] = grad
                    gains = gains + jnp.sum((up * scaled).reshape(B // 8, 8, B), axis=0)
                    lbuf[h, c] = later
                    later = kc_sm[c] * (tn(qh[h, c], grad) + later)
                gpart[h] = gains
                st2[h] = later.reshape(SHARDS, PIECE, B)

        loop(TILES // STEP, body)
        scatter(st2, rx2, s3, r3, g)

    for h in range(LOCAL):
        gain_tx[h : h + 1, :] = jnp.sum(gpart[h], axis=0, keepdims=True)

    for k in range(1, SHARDS):
        pltpu.make_async_remote_copy(
            gain_tx, gain_rx.at[me], gs.at[0], gr_sem.at[0],
            device_id={"ctx": lax.rem(me + k, SHARDS)}, device_id_type=MESH,
        ).start()
    gain_rx[me] = gain_tx[...]

    def pack(value, out, c):
        out[pl.ds(pl.multiple_of(c * B, B), B)] = jnp.swapaxes(value, 0, 1)

    def grad_q(g):
        def body(i):
            for n in range(STEP):
                c = i * STEP + n
                for h in range(g * G, (g + 1) * G):
                    grad = gh[h, c]
                    both = nt(grad, jnp.concatenate([vh[h, c], rbuf[h, c]], axis=0))
                    b = lower(both[:, :B])
                    bth[h, c] = turn(b)
                    rbuf[h, c] = (nn(b, kh[h, c]) + both[:, B:]).astype(BF16)

        loop(TILES // STEP, body)

    def put_normed(c):
        pack(ah[:, c], n_tok, c)

    loop(TILES, put_normed)
    for g in range(GROUPS):
        grad_q(g)
        chain(rx2, px2, inc2, r3, s4, r4, g, False)

    def put_dq(c):
        pack(rbuf[:, c], dq_tok, c)

    loop(TILES, put_dq)

    others = gain_rx.at[pl.ds(0, SHARDS - 1)]
    pltpu.make_async_copy(others, others, gr_sem.at[0]).wait()
    total = gain_rx[0]
    for k in range(1, SHARDS):
        total = total + gain_rx[k]
    dgain_ref[...] = total / math.sqrt(TOKENS)

    sent(rx, s1)
    sent(rx, s2)
    sent(rx, s3)
    sent(rx, s4)
    others = stat_rx.at[pl.ds(0, PEERS - 1)]
    pltpu.make_async_copy(others, others, hs.at[0]).wait()
    others = gain_rx.at[pl.ds(0, SHARDS - 1)]
    pltpu.make_async_copy(others, others, gs.at[0]).wait()
    for g in range(GROUPS):
        arrived(inc2, r4, g)


def finish(
    n_tok, dq_tok, qh, kh, vh, gh, ath, bth, lbuf, inc2, reach_ref, gain_sum,
    n_out, dq_out, dk_out, dv_out, gain_out,
    dk_tok, dv_tok, dkh, dvh, out_sem,
):
    whole = [
        pltpu.make_async_copy(n_tok, n_out, out_sem.at[0, 0]),
        pltpu.make_async_copy(dq_tok, dq_out, out_sem.at[1, 0]),
    ]
    for copy in whole:
        copy.start()
    def body(i):
        for n in range(PAIR):
            c = i * PAIR + n
            reach = reach_ref[pl.ds(c, 1), :]
            for h in range(LOCAL):
                leave = (lbuf[h, c] + reach * inc2[:, h].reshape(B, B)).astype(BF16)
                dk = nn(
                    jnp.concatenate([bth[h, c], vh[h, c]], axis=1),
                    jnp.concatenate([qh[h, c], turn(leave)], axis=0),
                )
                dv = nn(
                    jnp.concatenate([ath[h, c], kh[h, c]], axis=1),
                    jnp.concatenate([gh[h, c], leave], axis=0),
                )
                dkh[h, n] = dk.astype(BF16)
                dvh[h, n] = dv.astype(BF16)
        for n in range(PAIR):
            rows = pl.ds(pl.multiple_of((i * PAIR + n) * B, B), B)
            dk_tok[rows] = jnp.swapaxes(dkh[:, n], 0, 1)
            dv_tok[rows] = jnp.swapaxes(dvh[:, n], 0, 1)
        chunk_start(i)

    def chunk(stage, out, a, i):
        rows = pl.ds(i * PAIR * B, PAIR * B)
        return pltpu.make_async_copy(stage.at[rows], out.at[rows], out_sem.at[a, 1 + i])

    def chunk_start(i):
        chunk(dk_tok, dk_out, 0, i).start()
        chunk(dv_tok, dv_out, 1, i).start()

    loop(TILES // PAIR, body)
    gain_out[...] = gain_sum[...]
    for copy in whole:
        copy.wait()
    for i in range(TILES // PAIR):
        chunk(dk_tok, dk_out, 0, i).wait()
        chunk(dv_tok, dv_out, 1, i).wait()


def local(queries, key_rows, value_rows, grad_normed, norm_gain, document_starts):
    vmem = pl.BlockSpec(memory_space=pltpu.VMEM)
    tiles = (LOCAL, TILES, B, B)
    rows = (ROWS, LOCAL, HEAD_DIM)
    raw = pltpu.VMEM(rows, BF16)
    narrow = pltpu.VMEM(tiles, BF16)
    wide = pltpu.VMEM(tiles, F32)
    stats = pltpu.VMEM((TILES, B, B), F32)
    state = pltpu.VMEM((LOCAL, SHARDS, PIECE, B), F32)
    pieces = pltpu.VMEM((SHARDS, LOCAL, PIECE, B), F32)
    row = pltpu.VMEM((8, B), F32)
    hbm = pl.BlockSpec(memory_space=pltpu.HBM)
    dma = pltpu.SemaphoreType.DMA
    big = jax.ShapeDtypeStruct(rows, BF16)
    middle = pl.pallas_call(
        kernel,
        out_shape=(raw, raw, narrow, narrow, narrow, narrow, narrow, narrow, wide, pieces, row, row),
        in_specs=[hbm] * 6,
        out_specs=(vmem,) * 12,
        scratch_shapes=[row, pltpu.SMEM((6,), jnp.int32)]
        + [raw] * 4
        + [narrow, narrow, wide, narrow]
        + [stats] * 4
        + [pltpu.VMEM((LOCAL, 8, B), F32)]
        + [state, pieces, pieces, pieces, state, pieces, pieces]
        + [
            pltpu.VMEM((PEERS, 2, TILES, B), F32),
            pltpu.VMEM((2, TILES, B), F32),
            pltpu.VMEM((SHARDS, LOCAL, B), F32),
            pltpu.VMEM((LOCAL, B), F32),
        ]
        + [pltpu.SMEM((TILES,), F32)] * 2
        + [pltpu.SMEM((SHARDS,), F32)]
        + [dma((2,)), dma((4, 2))]
        + [dma((1,)), dma((GROUPS,))] * 4
        + [dma((1,))] * 4,
        compiler_params=pltpu.CompilerParams(
            collective_id=0, has_side_effects=True, vmem_limit_bytes=LIMIT
        ),
    )(queries, key_rows, value_rows, grad_normed, norm_gain, document_starts)
    pair = pltpu.VMEM((LOCAL, PAIR, B, B), BF16)
    grads = pl.pallas_call(
        finish,
        out_shape=(big,) * 4 + (jax.ShapeDtypeStruct((LOCAL, HEAD_DIM), F32),),
        in_specs=[vmem] * 12,
        out_specs=(hbm,) * 4 + (vmem,),
        scratch_shapes=[raw, raw, pair, pair]
        + [dma((2, 1 + TILES // PAIR))],
        compiler_params=pltpu.CompilerParams(vmem_limit_bytes=LIMIT2),
    )(*middle)
    return tuple(grads)


def solution(mesh):
    rows = P("ctx", "head", None)
    return jax.shard_map(
        local,
        mesh=mesh,
        in_specs=(rows, rows, rows, rows, P("head", None), P()),
        out_specs=(rows, rows, rows, rows, P("head", None)),
        check_vma=False,
    )
```

time: 74 us -> 55 us (0.74)
  Pallas kernels: 62.8 us -> 52.9 us
  local copies, waits for them, and re-layouts: 9.81 us -> 1.33 us
    pallas_call x1 -> x2, Pallas kernels: 62.8 us -> 52.9 us  [the longest x1 47.3 us: local(): pl.pallas_call(kernel, out_shape=(raw, raw, narrow, narrow, narrow, narro...]
    unnamed x13 -> x4, local copies, waits for them, and re-layouts: 9.81 us -> 1.33 us
where the time goes in v2:
time: 55 us; the launch traced here: 54.9 us
  Pallas kernels  52.9 us (96%)
  local copies, waits for them, and re-layouts  1.33 us (2%)
  between operations  0.65 us (1%)
    pallas_call x1, Pallas kernels, local(): pl.pallas_call(kernel, out_shape=(raw, raw, narrow, narrow, narrow, narro...  47.3 us
    pallas_call x1, Pallas kernels, local(): pl.pallas_call(finish, out_shape=(big,) * 4 + (jax.ShapeDtypeStruct((LOCA...  5.61 us
    unnamed x4, local copies, waits for them, and re-layouts  1.33 us

profile of v2, /device:TPU:0, one launch (start us, length us, event | category | flops | bytes accessed | tf_op | source)
XLA Modules:
  0.0 54.9 jit_solution(10985231852225431083)
XLA Ops:
  0.6 0.0 copy-start
  0.6 0.7 %copy-done = f32[8,128]{1,0:T(8,128)S(1)} copy-done((f32[8,128]{1,0:T(8,128)S(1)}, f32[8,128]{1,0:T(8,128)}, u32[]{:S(2)}) %copy-start) | copy-done | bytes 4120
  1.3 0.0 copy-start.1
  1.3 0.7 %copy-done.1 = s32[6]{0:T(128)S(1)} copy-done((s32[6]{0:T(128)S(1)}, s32[6]{0:T(128)}, u32[]{:S(2)}) %copy-start.1) | copy-done | bytes 48
  2.0 47.3 %shard_map.101 = (bf16[1024,8,128]{2,1,0:T(8,128)(2,1)S(1)}, bf16[1024,8,128]{2,1,0:T(8,128)(2,1)S(1)}, bf16[8,8,128,128]{3,2,1,0:T(8,128)(2,1)S(1)}, bf16[8,8,1...) custom-call(bf16[1024,8,128]{2,1,0:T(8,128)(2,1)} %q_hbm.1, ...), custom_call_target="tpu_custom_call" | custom-call | tf_op jit(solution)/shard_map/pallas_call | solution.py:454
  49.3 5.6 %shard_map.102 = (bf16[1024,8,128]{2,1,0:T(8,128)(2,1)}, bf16[1024,8,128]{2,1,0:T(8,128)(2,1)}, bf16[1024,8,128]{2,1,0:T(8,128)(2,1)}, bf16[1024,8,128]{2,1,0:T(8,128)(2,1)}, f32[8,128]{1,0:T(8,128)}) custom-call(bf16[1024,8,128]{2,1,0:T(8,128)(2,1)S(1)} %get-tuple-element.17.n_tok, bf16[1024,8,128]{2,1,0:T(8,128)(2,1)S(1)} %get-tuple-element.18.dq_tok, ...), custom_call_target="tpu_custom_call" | custom-call | tf_op jit(solution)/shard_map/pallas_call | solution.py:481
Async XLA Ops:
  0.6 0.7 %copy-start = (f32[8,128]{1,0:T(8,128)S(1)}, f32[8,128]{1,0:T(8,128)}, u32[]{:S(2)}) copy-start(f32[8,128]{1,0:T(8,128)} %gain_hbm.1) | copy-start | bytes 12292
  1.3 0.7 %copy-start.1 = (s32[6]{0:T(128)S(1)}, s32[6]{0:T(128)}, u32[]{:S(2)}) copy-start(s32[6]{0:T(128)} %starts_hbm.1) | copy-start | bytes 76

commit v3 on v2

--- a/solution.py
+++ b/solution.py
@@ -19,11 +19,11 @@
 B = 128
 TILES = ROWS // B
 HALF = ROWS // 2
-STEP = 4
+STEP = 8
 PAIR = 2
 LIMIT = 32 << 20
 LIMIT2 = 12 << 20
-GROUPS = 2
+GROUPS = 4
 G = LOCAL // GROUPS
 PIECE = HEAD_DIM // SHARDS
 MESH = pl.DeviceIdType.MESH
@@ -71,7 +71,7 @@
 
 def kernel(
     q_hbm, k_hbm, v_hbm, u_hbm, gain_hbm, starts_hbm,
-    n_tok, dq_tok, qh, kh, vh, gh, ath, bth, lbuf, inc2, reach_ref, dgain_ref,
+    n_tok, dq_tok, qh, kh, vh, gh, ath, bth, lbuf, inc2, dkh, dvh, reach_ref, dgain_ref,
     gain_ref, starts_ref, q_raw, k_raw, v_raw, u_raw,
     uh, ah, att, rbuf,
     sqa, cra, invb, cob, gpart,
@@ -175,27 +175,17 @@
 
     def chain(rx, px, inc, r_in, s_out, r_out, g, forward):
         arrived(rx, r_in, g)
-        first = 0 if forward else SHARDS - 1
-        px[first, group(g)] = jnp.zeros((G, PIECE, B), F32)
-
-        def step(turn, total):
-            i = turn if forward else SHARDS - 1 - turn
+        order = list(range(SHARDS)) if forward else list(reversed(range(SHARDS)))
+        total = jnp.zeros((G, PIECE, B), F32)
+        for i in order:
+            px[i, group(g)] = total
             total = rx[i, group(g)] + keep_sm[i] * total
-
-            @pl.when(turn < SHARDS - 1)
-            def _():
-                px[i + 1 if forward else i - 1, group(g)] = total
-
-            @pl.when(i != me)
-            def _():
-                pltpu.make_async_remote_copy(
-                    px.at[i, group(g)], inc.at[me, group(g)], s_out.at[0], r_out.at[g],
-                    device_id={"ctx": i}, device_id_type=MESH,
-                ).start()
-
-            return total
-
-        lax.fori_loop(0, SHARDS, step, jnp.zeros((G, PIECE, B), F32))
+        for o in OFFSETS:
+            i = at_offset(o)
+            pltpu.make_async_remote_copy(
+                px.at[i, group(g)], inc.at[me, group(g)], s_out.at[0], r_out.at[g],
+                device_id={"ctx": i}, device_id_type=MESH,
+            ).start()
         inc[me, group(g)] = px[me, group(g)]
 
     def arrived(dst, rsem, g):
@@ -342,16 +332,27 @@
     def pack(value, out, c):
         out[pl.ds(pl.multiple_of(c * B, B), B)] = jnp.swapaxes(value, 0, 1)
 
+    def grad_scores(g):
+        def body(i):
+            for n in range(STEP):
+                c = i * STEP + n
+                for h in range(g * G, (g + 1) * G):
+                    b = lower(nt(gh[h, c], vh[h, c]))
+                    ah[h, c] = b
+                    bth[h, c] = turn(b)
+
+        loop(TILES // STEP, body)
+
     def grad_q(g):
         def body(i):
             for n in range(STEP):
                 c = i * STEP + n
                 for h in range(g * G, (g + 1) * G):
-                    grad = gh[h, c]
-                    both = nt(grad, jnp.concatenate([vh[h, c], rbuf[h, c]], axis=0))
-                    b = lower(both[:, :B])
-                    bth[h, c] = turn(b)
-                    rbuf[h, c] = (nn(b, kh[h, c]) + both[:, B:]).astype(BF16)
+                    dq = nn(
+                        jnp.concatenate([ah[h, c], gh[h, c]], axis=1),
+                        jnp.concatenate([kh[h, c], turn(rbuf[h, c])], axis=0),
+                    )
+                    uh[h, c] = dq.astype(BF16)
 
         loop(TILES // STEP, body)
 
@@ -360,11 +361,16 @@
 
     loop(TILES, put_normed)
     for g in range(GROUPS):
+        grad_scores(g)
+        if g >= 1:
+            chain(rx2, px2, inc2, r3, s4, r4, g - 1, False)
+    grad_q(0)
+    chain(rx2, px2, inc2, r3, s4, r4, GROUPS - 1, False)
+    for g in range(1, GROUPS):
         grad_q(g)
-        chain(rx2, px2, inc2, r3, s4, r4, g, False)
 
     def put_dq(c):
-        pack(rbuf[:, c], dq_tok, c)
+        pack(uh[:, c], dq_tok, c)
 
     loop(TILES, put_dq)
 
@@ -374,6 +380,19 @@
     for k in range(1, SHARDS):
         total = total + gain_rx[k]
     dgain_ref[...] = total / math.sqrt(TOKENS)
+
+    for g in range(GROUPS - 1):
+        arrived(inc2, r4, g)
+
+        def body(i, g=g):
+            for n in range(STEP):
+                c = i * STEP + n
+                for h in range(g * G, (g + 1) * G):
+                    dk, dv = tail(qh, kh, vh, gh, ath, bth, lbuf, inc2, reach_ref, h, c)
+                    dkh[h, c] = dk
+                    dvh[h, c] = dv
+
+        loop(TILES // STEP, body)
 
     sent(rx, s1)
     sent(rx, s2)
@@ -383,14 +402,27 @@
     pltpu.make_async_copy(others, others, hs.at[0]).wait()
     others = gain_rx.at[pl.ds(0, SHARDS - 1)]
     pltpu.make_async_copy(others, others, gs.at[0]).wait()
-    for g in range(GROUPS):
-        arrived(inc2, r4, g)
+    arrived(inc2, r4, GROUPS - 1)
+
+
+def tail(qh, kh, vh, gh, ath, bth, lbuf, inc2, reach_ref, h, c):
+    reach = reach_ref[pl.ds(c, 1), :]
+    leave = (lbuf[h, c] + reach * inc2[:, h].reshape(B, B)).astype(BF16)
+    dk = nn(
+        jnp.concatenate([bth[h, c], vh[h, c]], axis=1),
+        jnp.concatenate([qh[h, c], turn(leave)], axis=0),
+    )
+    dv = nn(
+        jnp.concatenate([ath[h, c], kh[h, c]], axis=1),
+        jnp.concatenate([gh[h, c], leave], axis=0),
+    )
+    return dk.astype(BF16), dv.astype(BF16)
 
 
 def finish(
-    n_tok, dq_tok, qh, kh, vh, gh, ath, bth, lbuf, inc2, reach_ref, gain_sum,
+    n_tok, dq_tok, qh, kh, vh, gh, ath, bth, lbuf, inc2, dkh, dvh, reach_ref, gain_sum,
     n_out, dq_out, dk_out, dv_out, gain_out,
-    dk_tok, dv_tok, dkh, dvh, out_sem,
+    dk_tok, dv_tok, dk_last, dv_last, out_sem,
 ):
     whole = [
         pltpu.make_async_copy(n_tok, n_out, out_sem.at[0, 0]),
@@ -398,26 +430,24 @@
     ]
     for copy in whole:
         copy.start()
+    first = LOCAL - G
+    for c in range(TILES):
+        for h in range(G):
+            dk, dv = tail(
+                qh, kh, vh, gh, ath, bth, lbuf, inc2, reach_ref, first + h, c
+            )
+            dk_last[h, c] = dk
+            dv_last[h, c] = dv
+
+    def pack(head, last, out, c):
+        rows = pl.ds(pl.multiple_of(c * B, B), B)
+        whole = jnp.concatenate([head[:first, c], last[:, c]], axis=0)
+        out[rows] = jnp.swapaxes(whole, 0, 1)
+
     def body(i):
         for n in range(PAIR):
-            c = i * PAIR + n
-            reach = reach_ref[pl.ds(c, 1), :]
-            for h in range(LOCAL):
-                leave = (lbuf[h, c] + reach * inc2[:, h].reshape(B, B)).astype(BF16)
-                dk = nn(
-                    jnp.concatenate([bth[h, c], vh[h, c]], axis=1),
-                    jnp.concatenate([qh[h, c], turn(leave)], axis=0),
-                )
-                dv = nn(
-                    jnp.concatenate([ath[h, c], kh[h, c]], axis=1),
-                    jnp.concatenate([gh[h, c], leave], axis=0),
-                )
-                dkh[h, n] = dk.astype(BF16)
-                dvh[h, n] = dv.astype(BF16)
-        for n in range(PAIR):
-            rows = pl.ds(pl.multiple_of((i * PAIR + n) * B, B), B)
-            dk_tok[rows] = jnp.swapaxes(dkh[:, n], 0, 1)
-            dv_tok[rows] = jnp.swapaxes(dvh[:, n], 0, 1)
+            pack(dkh, dk_last, dk_tok, i * PAIR + n)
+            pack(dvh, dv_last, dv_tok, i * PAIR + n)
         chunk_start(i)
 
     def chunk(stage, out, a, i):
@@ -453,9 +483,10 @@
     big = jax.ShapeDtypeStruct(rows, BF16)
     middle = pl.pallas_call(
         kernel,
-        out_shape=(raw, raw, narrow, narrow, narrow, narrow, narrow, narrow, wide, pieces, row, row),
+        out_shape=(raw, raw, narrow, narrow, narrow, narrow, narrow, narrow, wide, pieces)
+        + (narrow, narrow, row, row),
         in_specs=[hbm] * 6,
-        out_specs=(vmem,) * 12,
+        out_specs=(vmem,) * 14,
         scratch_shapes=[row, pltpu.SMEM((6,), jnp.int32)]
         + [raw] * 4
         + [narrow, narrow, wide, narrow]
@@ -476,12 +507,12 @@
         compiler_params=pltpu.CompilerParams(
             collective_id=0, has_side_effects=True, vmem_limit_bytes=LIMIT
         ),
-    )(queries, key_rows, value_rows, grad_normed, norm_gain, document_starts)
-    pair = pltpu.VMEM((LOCAL, PAIR, B, B), BF16)
+    )(queries, key_rows, value_rows, grad_normed, *(pltpu.with_memory_space_constraint(a, pltpu.HBM) for a in (norm_gain, document_starts)))
+    pair = pltpu.VMEM((G, TILES, B, B), BF16)
     grads = pl.pallas_call(
         finish,
         out_shape=(big,) * 4 + (jax.ShapeDtypeStruct((LOCAL, HEAD_DIM), F32),),
-        in_specs=[vmem] * 12,
+        in_specs=[vmem] * 14,
         out_specs=(hbm,) * 4 + (vmem,),
         scratch_shapes=[raw, raw, pair, pair]
         + [dma((2, 1 + TILES // PAIR))],

time: 55 us -> 50.2 us (0.913)
  Pallas kernels: 52.9 us -> 49.1 us
  local copies, waits for them, and re-layouts: 1.33 us -> 0 us
    pallas_call x1, Pallas kernels: 47.3 us -> 44.6 us  [local(): pl.pallas_call(kernel, out_shape=(raw, raw, narrow, narrow, narrow, narro...]
    unnamed x4 -> x0, local copies, waits for them, and re-layouts: 1.33 us -> none
    pallas_call x1, Pallas kernels: 5.61 us -> 4.52 us  [local(): pl.pallas_call(finish, out_shape=(big,) * 4 + (jax.ShapeDtypeStruct((LOCA...]
where the time goes in v3:
time: 50.2 us; the launch traced here: 49.9 us
  Pallas kernels  49.1 us (98%)
  between operations  0.8 us (2%)
    pallas_call x1, Pallas kernels, local(): pl.pallas_call(kernel, out_shape=(raw, raw, narrow, narrow, narrow, narro...  44.6 us
    pallas_call x1, Pallas kernels, local(): pl.pallas_call(finish, out_shape=(big,) * 4 + (jax.ShapeDtypeStruct((LOCA...  4.52 us

profile of v3, /device:TPU:0, one launch (start us, length us, event | category | flops | bytes accessed | tf_op | source)
XLA Modules:
  0.0 49.9 jit_solution(6526521489343607288)
XLA Ops:
  0.6 44.6 %shard_map.101 = (bf16[1024,8,128]{2,1,0:T(8,128)(2,1)S(1)}, bf16[1024,8,128]{2,1,0:T(8,128)(2,1)S(1)}, bf16[8,8,128,128]{3,2,1,0:T(8,128)(2,1)S(1)}, bf16[8,8,1...) custom-call(bf16[1024,8,128]{2,1,0:T(8,128)(2,1)} %q_hbm.1, ...), custom_call_target="tpu_custom_call" | custom-call | tf_op jit(solution)/shard_map/pallas_call | solution.py:484
  45.2 4.5 %shard_map.102 = (bf16[1024,8,128]{2,1,0:T(8,128)(2,1)}, bf16[1024,8,128]{2,1,0:T(8,128)(2,1)}, bf16[1024,8,128]{2,1,0:T(8,128)(2,1)}, bf16[1024,8,128]{2,1,0:T(8,128)(2,1)}, f32[8,128]{1,0:T(8,128)}) custom-call(bf16[1024,8,128]{2,1,0:T(8,128)(2,1)S(1)} %get-tuple-element.19.n_tok, bf16[1024,8,128]{2,1,0:T(8,128)(2,1)S(1)} %get-tuple-element.20.dq_tok, ...), custom_call_target="tpu_custom_call" | custom-call | tf_op jit(solution)/shard_map/pallas_call | solution.py:512

commit v4 on v3

--- a/solution.py
+++ b/solution.py
@@ -21,6 +21,7 @@
 HALF = ROWS // 2
 STEP = 8
 PAIR = 2
+ROWS_STEP = 32
 LIMIT = 32 << 20
 LIMIT2 = 12 << 20
 GROUPS = 4
@@ -52,6 +53,9 @@
 
 
 def loop(count, body):
+    if count == 1:
+        return body(0)
+
     def step(i, carry):
         body(i)
         return carry
@@ -76,7 +80,7 @@
     uh, ah, att, rbuf,
     sqa, cra, invb, cob, gpart,
     st, rx, px, inc, st2, rx2, px2,
-    stat_rx, stat_tx, gain_rx, gain_tx,
+    stat_rx, stat_tx, gain_rx, gain_tx, gain_sum, gain_all,
     kc_sm, mp_sm, keep_sm,
     small_sem, in_sem, s1, r1, s2, r2, s3, r3, s4, r4, hs, hr, gs, gr_sem,
 ):
@@ -86,6 +90,16 @@
 
     def at_offset(o):
         return lax.rem(y + o // 4, 4) * 4 + lax.rem(z + o % 4, 4)
+
+    barrier = pltpu.get_barrier_semaphore()
+    for o in OFFSETS:
+        pl.semaphore_signal(
+            barrier, inc=1, device_id={"ctx": at_offset(o)}, device_id_type=MESH
+        )
+    for k in range(1, PEERS):
+        pl.semaphore_signal(
+            barrier, inc=1, device_id={"head": lax.rem(my_head + k, PEERS)}, device_id_type=MESH
+        )
 
     hbm_in = (k_hbm, v_hbm, q_hbm, u_hbm)
     raw_in = (k_raw, v_raw, q_raw, u_raw)
@@ -104,16 +118,6 @@
         for c in range(2):
             load(a, c).start()
             load(b, c).start()
-
-    barrier = pltpu.get_barrier_semaphore()
-    for k in range(1, SHARDS):
-        pl.semaphore_signal(
-            barrier, inc=1, device_id={"ctx": lax.rem(me + k, SHARDS)}, device_id_type=MESH
-        )
-    for k in range(1, PEERS):
-        pl.semaphore_signal(
-            barrier, inc=1, device_id={"head": lax.rem(my_head + k, PEERS)}, device_id_type=MESH
-        )
 
     for copy in small:
         copy.wait()
@@ -210,11 +214,10 @@
         load(1, half).wait()
         unpack_half(v_raw, vh, half)
 
-    states(0)
+    for g in range(GROUPS):
+        states(g)
     pl.semaphore_wait(barrier, SHARDS - 1 + PEERS - 1)
-    scatter(st, rx, s1, r1, 0)
-    for g in range(1, GROUPS):
-        states(g)
+    for g in range(GROUPS):
         scatter(st, rx, s1, r1, g)
 
     for half in range(2):
@@ -240,35 +243,31 @@
         if g + 1 < GROUPS:
             scores(g + 1)
 
+    sq_cols = jnp.zeros((B, B), F32)
+    cr_cols = jnp.zeros((B, B), F32)
     for g in range(GROUPS):
         arrived(inc, r2, g)
-
-        def body(i, g=g):
-            for n in range(STEP):
-                c = i * STEP + n
-                sq = jnp.zeros((B, B), F32) if g == 0 else sqa[c]
-                cr = jnp.zeros((B, B), F32) if g == 0 else cra[c]
-                reach = mp_sm[c]
-                for h in range(g * G, (g + 1) * G):
-                    entry = (lbuf[h, c] + reach * inc[:, h].reshape(B, B)).astype(BF16)
-                    rbuf[h, c] = entry
-                    out = nn(
-                        jnp.concatenate([ah[h, c], qh[h, c]], axis=1),
-                        jnp.concatenate([vh[h, c], entry], axis=0),
-                    )
-                    att[h, c] = out
-                    sq = sq + out * out
-                    cr = cr + uh[h, c].astype(F32) * gain_ref[h : h + 1, :] * out
+        for c in range(TILES):
+            sq = jnp.zeros((B, B), F32) if g == 0 else sqa[c]
+            cr = jnp.zeros((B, B), F32) if g == 0 else cra[c]
+            reach = mp_sm[c]
+            for h in range(g * G, (g + 1) * G):
+                entry = (lbuf[h, c] + reach * inc[:, h].reshape(B, B)).astype(BF16)
+                rbuf[h, c] = entry
+                out = nn(
+                    jnp.concatenate([ah[h, c], qh[h, c]], axis=1),
+                    jnp.concatenate([vh[h, c], entry], axis=0),
+                )
+                att[h, c] = out
+                sq = sq + out * out
+                cr = cr + uh[h, c].astype(F32) * gain_ref[h : h + 1, :] * out
+            if g < GROUPS - 1:
                 sqa[c] = sq
                 cra[c] = cr
-
-        loop(TILES // STEP, body)
-
-    sq_cols = jnp.zeros((B, B), F32)
-    cr_cols = jnp.zeros((B, B), F32)
-    for c in range(TILES):
-        sq_cols = jnp.where(col == c, jnp.sum(sqa[c], axis=1, keepdims=True), sq_cols)
-        cr_cols = jnp.where(col == c, jnp.sum(cra[c], axis=1, keepdims=True), cr_cols)
+            else:
+                sq_cols = jnp.where(col == c, jnp.sum(sq, axis=1, keepdims=True), sq_cols)
+                cr_cols = jnp.where(col == c, jnp.sum(cr, axis=1, keepdims=True), cr_cols)
+
     stat_tx[0] = jnp.transpose(sq_cols)[:TILES]
     stat_tx[1] = jnp.transpose(cr_cols)[:TILES]
 
@@ -303,16 +302,20 @@
                 gains = gpart[h]
                 for n in range(STEP):
                     c = TILES - 1 - (i * STEP + n)
-                    inv = invb[c]
-                    out = att[h, c]
-                    up = uh[h, c].astype(F32)
-                    scaled = out * inv
-                    ah[h, c] = (scaled * gain).astype(BF16)
-                    grad = (inv * (up * gain) - out * cob[c]).astype(BF16)
-                    gh[h, c] = grad
-                    gains = gains + jnp.sum((up * scaled).reshape(B // 8, 8, B), axis=0)
+                    for r in range(0, B, ROWS_STEP):
+                        part = slice(r, r + ROWS_STEP)
+                        inv = invb[c, part]
+                        out = att[h, c, part]
+                        up = uh[h, c, part].astype(F32)
+                        scaled = out * inv
+                        ah[h, c, part] = (scaled * gain).astype(BF16)
+                        grad = inv * (up * gain) - out * cob[c, part]
+                        gh[h, c, part] = grad.astype(BF16)
+                        gains = gains + jnp.sum(
+                            (up * scaled).reshape(ROWS_STEP // 8, 8, B), axis=0
+                        )
                     lbuf[h, c] = later
-                    later = kc_sm[c] * (tn(qh[h, c], grad) + later)
+                    later = kc_sm[c] * (tn(qh[h, c], gh[h, c]) + later)
                 gpart[h] = gains
                 st2[h] = later.reshape(SHARDS, PIECE, B)
 
@@ -320,14 +323,53 @@
         scatter(st2, rx2, s3, r3, g)
 
     for h in range(LOCAL):
-        gain_tx[h : h + 1, :] = jnp.sum(gpart[h], axis=0, keepdims=True)
-
-    for k in range(1, SHARDS):
-        pltpu.make_async_remote_copy(
-            gain_tx, gain_rx.at[me], gs.at[0], gr_sem.at[0],
-            device_id={"ctx": lax.rem(me + k, SHARDS)}, device_id_type=MESH,
-        ).start()
-    gain_rx[me] = gain_tx[...]
+        gain_tx[h] = jnp.sum(gpart[h], axis=0, keepdims=True)
+
+        @pl.when(me != h)
+        def _(h=h):
+            pltpu.make_async_remote_copy(
+                gain_tx.at[h], gain_rx.at[me], gs.at[0], gr_sem.at[0],
+                device_id={"ctx": h}, device_id_type=MESH,
+            ).start()
+
+        @pl.when(me == h)
+        def _(h=h):
+            gain_rx[me] = gain_tx[h]
+
+    def rows_wait(buffer, count, sem):
+        some = buffer.at[pl.ds(0, count)]
+        pltpu.make_async_copy(some, some, sem).wait()
+
+    def gain_sums():
+        @pl.when(me < LOCAL)
+        def _():
+            rows_wait(gain_rx, SHARDS - 1, gr_sem.at[0])
+            total = gain_rx[0]
+            for k in range(1, SHARDS):
+                total = total + gain_rx[k]
+            total = total / math.sqrt(TOKENS)
+            gain_sum[...] = total
+            gain_all[me] = total
+            for o in OFFSETS:
+                pltpu.make_async_remote_copy(
+                    gain_sum, gain_all.at[me], gs.at[1], gr_sem.at[1],
+                    device_id={"ctx": at_offset(o)}, device_id_type=MESH,
+                ).start()
+
+    def gain_done():
+        @pl.when(me < LOCAL)
+        def _():
+            rows_wait(gain_all, LOCAL - 1, gr_sem.at[1])
+            rows_wait(gain_all, LOCAL - 1, gs.at[0])
+            rows_wait(gain_rx, SHARDS - 1, gs.at[1])
+
+        @pl.when(me >= LOCAL)
+        def _():
+            rows_wait(gain_all, LOCAL, gr_sem.at[1])
+            rows_wait(gain_all, LOCAL, gs.at[0])
+
+        for h in range(LOCAL):
+            dgain_ref[h : h + 1, :] = gain_all[h]
 
     def pack(value, out, c):
         out[pl.ds(pl.multiple_of(c * B, B), B)] = jnp.swapaxes(value, 0, 1)
@@ -364,22 +406,18 @@
         grad_scores(g)
         if g >= 1:
             chain(rx2, px2, inc2, r3, s4, r4, g - 1, False)
-    grad_q(0)
+        if g == GROUPS - 1:
+            gain_sums()
+    for g in range(GROUPS // 2):
+        grad_q(g)
     chain(rx2, px2, inc2, r3, s4, r4, GROUPS - 1, False)
-    for g in range(1, GROUPS):
+    for g in range(GROUPS // 2, GROUPS):
         grad_q(g)
 
     def put_dq(c):
         pack(uh[:, c], dq_tok, c)
 
     loop(TILES, put_dq)
-
-    others = gain_rx.at[pl.ds(0, SHARDS - 1)]
-    pltpu.make_async_copy(others, others, gr_sem.at[0]).wait()
-    total = gain_rx[0]
-    for k in range(1, SHARDS):
-        total = total + gain_rx[k]
-    dgain_ref[...] = total / math.sqrt(TOKENS)
 
     for g in range(GROUPS - 1):
         arrived(inc2, r4, g)
@@ -400,8 +438,7 @@
     sent(rx, s4)
     others = stat_rx.at[pl.ds(0, PEERS - 1)]
     pltpu.make_async_copy(others, others, hs.at[0]).wait()
-    others = gain_rx.at[pl.ds(0, SHARDS - 1)]
-    pltpu.make_async_copy(others, others, gs.at[0]).wait()
+    gain_done()
     arrived(inc2, r4, GROUPS - 1)
 
 
@@ -431,34 +468,37 @@
     for copy in whole:
         copy.start()
     first = LOCAL - G
-    for c in range(TILES):
-        for h in range(G):
-            dk, dv = tail(
-                qh, kh, vh, gh, ath, bth, lbuf, inc2, reach_ref, first + h, c
-            )
-            dk_last[h, c] = dk
-            dv_last[h, c] = dv
+
+    def last_group(i):
+        for c in range(i * PAIR, (i + 1) * PAIR):
+            for h in range(G):
+                dk, dv = tail(
+                    qh, kh, vh, gh, ath, bth, lbuf, inc2, reach_ref, first + h, c
+                )
+                dk_last[h, c] = dk
+                dv_last[h, c] = dv
 
     def pack(head, last, out, c):
-        rows = pl.ds(pl.multiple_of(c * B, B), B)
+        rows = pl.ds(c * B, B)
         whole = jnp.concatenate([head[:first, c], last[:, c]], axis=0)
         out[rows] = jnp.swapaxes(whole, 0, 1)
 
-    def body(i):
+    def chunk(stage, out, a, i):
+        rows = pl.ds(i * PAIR * B, PAIR * B)
+        return pltpu.make_async_copy(stage.at[rows], out.at[rows], out_sem.at[a, 1 + i])
+
+    def chunk_start(i):
+        chunk(dk_tok, dk_out, 0, i).start()
+        chunk(dv_tok, dv_out, 1, i).start()
+
+    last_group(0)
+    for i in range(TILES // PAIR):
+        if i + 1 < TILES // PAIR:
+            last_group(i + 1)
         for n in range(PAIR):
             pack(dkh, dk_last, dk_tok, i * PAIR + n)
             pack(dvh, dv_last, dv_tok, i * PAIR + n)
         chunk_start(i)
-
-    def chunk(stage, out, a, i):
-        rows = pl.ds(i * PAIR * B, PAIR * B)
-        return pltpu.make_async_copy(stage.at[rows], out.at[rows], out_sem.at[a, 1 + i])
-
-    def chunk_start(i):
-        chunk(dk_tok, dk_out, 0, i).start()
-        chunk(dv_tok, dv_out, 1, i).start()
-
-    loop(TILES // PAIR, body)
     gain_out[...] = gain_sum[...]
     for copy in whole:
         copy.wait()
@@ -496,14 +536,17 @@
         + [
             pltpu.VMEM((PEERS, 2, TILES, B), F32),
             pltpu.VMEM((2, TILES, B), F32),
-            pltpu.VMEM((SHARDS, LOCAL, B), F32),
-            pltpu.VMEM((LOCAL, B), F32),
+            pltpu.VMEM((SHARDS, 1, B), F32),
+            pltpu.VMEM((LOCAL, 1, B), F32),
+            pltpu.VMEM((1, B), F32),
+            pltpu.VMEM((LOCAL, 1, B), F32),
         ]
         + [pltpu.SMEM((TILES,), F32)] * 2
         + [pltpu.SMEM((SHARDS,), F32)]
         + [dma((2,)), dma((4, 2))]
         + [dma((1,)), dma((GROUPS,))] * 4
-        + [dma((1,))] * 4,
+        + [dma((1,))] * 2
+        + [dma((2,))] * 2,
         compiler_params=pltpu.CompilerParams(
             collective_id=0, has_side_effects=True, vmem_limit_bytes=LIMIT
         ),

time: 50.2 us -> 49.9 us (level)
  no operation moved by 1% of the time
where the time goes in v4:
time: 49.9 us; the launch traced here: 49.8 us
  Pallas kernels  49 us (98%)
  between operations  0.8 us (2%)
    pallas_call x1, Pallas kernels, local(): pl.pallas_call(kernel, out_shape=(raw, raw, narrow, narrow, narrow, narro...  44.5 us
    pallas_call x1, Pallas kernels, local(): pl.pallas_call(finish, out_shape=(big,) * 4 + (jax.ShapeDtypeStruct((LOCA...  4.42 us

profile of v4, /device:TPU:0, one launch (start us, length us, event | category | flops | bytes accessed | tf_op | source)
XLA Modules:
  0.0 49.8 jit_solution(17662610974274180696)
XLA Ops:
  0.6 44.5 %shard_map.101 = (bf16[1024,8,128]{2,1,0:T(8,128)(2,1)S(1)}, bf16[1024,8,128]{2,1,0:T(8,128)(2,1)S(1)}, bf16[8,8,128,128]{3,2,1,0:T(8,128)(2,1)S(1)}, bf16[8,8,1...) custom-call(bf16[1024,8,128]{2,1,0:T(8,128)(2,1)} %q_hbm.1, ...), custom_call_target="tpu_custom_call" | custom-call | tf_op jit(solution)/shard_map/pallas_call | solution.py:524
  45.2 4.4 %shard_map.102 = (bf16[1024,8,128]{2,1,0:T(8,128)(2,1)}, bf16[1024,8,128]{2,1,0:T(8,128)(2,1)}, bf16[1024,8,128]{2,1,0:T(8,128)(2,1)}, bf16[1024,8,128]{2,1,0:T(8,128)(2,1)}, f32[8,128]{1,0:T(8,128)}) custom-call(bf16[1024,8,128]{2,1,0:T(8,128)(2,1)S(1)} %get-tuple-element.19.n_tok, bf16[1024,8,128]{2,1,0:T(8,128)(2,1)S(1)} %get-tuple-element.20.dq_tok, ...), custom_call_target="tpu_custom_call" | custom-call | tf_op jit(solution)/shard_map/pallas_call | solution.py:555
